TPU v7x, 256 devices: a whole 4x4x8 slice. The times are simulated.
256 devices in a mesh: section: 4 (over y), seq: 32 (over z, x), head: 2 (over core).
Axes of the slice: x: 4, y: 4, z: 8, core: 2. Of those that a mesh axis runs over, the one named last changes fastest.
Arguments:
- queries: bfloat16 [32768, 4096], P(('section', 'seq'), 'head'), may hold values from -180 to 180
- keys: bfloat16 [32768, 1024], P(('section', 'seq'), 'head'), may hold values from -6 to 6
- values: bfloat16 [32768, 1024], P(('section', 'seq'), 'head'), may hold values from -6 to 6
- query_pooling_weight: float32 [4, 4096], P(None, 'head'), may hold values from -3 to 3
- key_pooling_weight: float32 [4, 1024], P(None, 'head'), may hold values from -3 to 3
- value_pooling_weight: float32 [4, 1024], P(None, 'head'), may hold values from -3 to 3
- up_weight: float32 [4, 4096], P(None, 'head'), may hold values from -8 to 8
- out_gain: float32 [4096], P('head'), may hold values from 0.1 to 1.9
Outputs:
- attended: bfloat16 [32768, 4096], P(('section', 'seq'), 'head')
All inputs are finite; a program needn't handle non-finite values.
Results may differ from a plain program's by a relative error of at most 0.0067.
Values may be sent and summed in bfloat16 or wider, within the bound.
A program may use at most 128 MiB of HBM per device.

v0:
```python
import jax
import jax.numpy as jnp
from jax import lax
from jax.sharding import PartitionSpec as P

HEAD_SIZE = 128
D = 4096
POOL_FACTOR = 4
WINDOW_LENGTH = 512


def passed_along(value, axis, steps):
    count = lax.axis_size(axis)
    initial, last = (max(0, -steps), min(count, count - steps))
    return lax.ppermute(value, axis, [(source, source + steps) for source in range(initial, last)])


def pool_rows(source, weights):
    grouped = source.reshape(source.shape[0] // weights.shape[0], weights.shape[0], source.shape[1])
    return jnp.sum(grouped * weights[None], axis=1).astype(jnp.bfloat16)


def window_attention(queries, keys_all, values_all, first_token, reach_count):
    tokens = queries.shape[0]
    kv_heads = keys_all.shape[1] // HEAD_SIZE
    group_length = queries.shape[1] // (kv_heads * HEAD_SIZE)
    shaped_q = queries.reshape(tokens, kv_heads, group_length, HEAD_SIZE)
    shaped_k = keys_all.reshape(-1, kv_heads, HEAD_SIZE)
    shaped_v = values_all.reshape(-1, kv_heads, HEAD_SIZE)
    scores = jnp.einsum(
        "qhgd,khd->hgqk", shaped_q, shaped_k, preferred_element_type=jnp.float32
    ) * HEAD_SIZE ** (-0.5)
    query_pos = first_token + jnp.arange(tokens)
    key_pos = first_token - reach_count * tokens + jnp.arange(keys_all.shape[0])
    allowed = (
        (key_pos[None, :] <= query_pos[:, None])
        & (key_pos[None, :] > query_pos[:, None] - WINDOW_LENGTH)
        & (key_pos[None, :] >= 0)
    )
    scores = jnp.where(allowed, scores, -jnp.inf)
    highest = jnp.max(scores, axis=-1, keepdims=True)
    weights = jnp.exp(scores - highest)
    normalizer = jnp.sum(weights, axis=-1)
    blended = jnp.einsum(
        "hgqk,khd->qhgd", weights.astype(jnp.bfloat16), shaped_v, preferred_element_type=jnp.float32
    )
    return (blended / jnp.transpose(normalizer, (2, 0, 1))[..., None]).reshape(tokens, -1)


def empty_state(query_count, kv_heads, group_length):
    running_max = jnp.full((kv_heads, group_length, query_count), -jnp.inf, jnp.float32)
    running_sum = jnp.zeros((kv_heads, group_length, query_count), jnp.float32)
    running_acc = jnp.zeros((kv_heads, group_length, query_count, HEAD_SIZE), jnp.float32)
    return (running_max, running_sum, running_acc)


def coarse_update(state, query_rows, query_pos, block_keys, block_values, key_pos):
    running_max, running_sum, running_acc = state
    kv_heads = block_keys.shape[1] // HEAD_SIZE
    group_length = query_rows.shape[1] // (kv_heads * HEAD_SIZE)
    shaped_q = query_rows.reshape(query_rows.shape[0], kv_heads, group_length, HEAD_SIZE)
    shaped_k = block_keys.reshape(-1, kv_heads, HEAD_SIZE)
    shaped_v = block_values.reshape(-1, kv_heads, HEAD_SIZE)
    scores = jnp.einsum(
        "qhgd,khd->hgqk", shaped_q, shaped_k, preferred_element_type=jnp.float32
    ) * HEAD_SIZE ** (-0.5)
    scores = jnp.where(key_pos[None, :] <= query_pos[:, None], scores, -jnp.inf)
    newest = jnp.maximum(running_max, jnp.max(scores, axis=-1))
    anchor = jnp.where(newest == -jnp.inf, 0.0, newest)
    weights = jnp.exp(scores - anchor[..., None])
    rescale = jnp.exp(running_max - anchor)
    running_sum = running_sum * rescale + jnp.sum(weights, axis=-1)
    running_acc = running_acc * rescale[..., None] + jnp.einsum(
        "hgqk,khd->hgqd", weights.astype(jnp.bfloat16), shaped_v, preferred_element_type=jnp.float32
    )
    return (newest, running_sum, running_acc)


def guarded_update(single, query_rows, query_pos, block_keys, block_values, key_pos):

    def update_state(carried):
        return coarse_update(carried, query_rows, query_pos, block_keys, block_values, key_pos)

    def keep_state(carried):
        return carried

    return lax.cond(jnp.min(key_pos) <= jnp.max(query_pos), update_state, keep_state, single)


def fold_blocks(state_sets, piece, query_sets, position_fn):
    piece_keys, piece_values = piece
    row_count = piece_keys.shape[0]
    block_rows = row_count
    while block_rows > 2048 and block_rows % 2 == 0:
        block_rows = block_rows // 2
    block_count = row_count // block_rows

    def one_block(step_index, states):
        starting_row = step_index * block_rows
        block_keys = lax.dynamic_slice_in_dim(piece_keys, starting_row, block_rows, 0)
        block_values = lax.dynamic_slice_in_dim(piece_values, starting_row, block_rows, 0)
        key_pos = position_fn(starting_row + jnp.arange(block_rows))
        updated = []
        for query_set, single in zip(query_sets, states):
            updated.append(
                guarded_update(
                    single, query_set[0], query_set[1], block_keys, block_values, key_pos
                )
            )
        return tuple(updated)

    return lax.fori_loop(0, block_count, one_block, state_sets)


def finish_state(state):
    running_max, running_sum, running_acc = state
    safe_sum = jnp.where(running_sum > 0.0, running_sum, 1.0)
    result = running_acc / safe_sum[..., None]
    return jnp.transpose(result, (2, 0, 1, 3)).reshape(result.shape[2], -1)


def same_position(global_rows):
    return global_rows


def per_device(
    queries,
    keys,
    values,
    query_pooling_weight,
    key_pooling_weight,
    value_pooling_weight,
    up_weight,
    out_gain,
):
    tokens = queries.shape[0]
    pooled_rows = tokens // POOL_FACTOR
    kv_heads = keys.shape[1] // HEAD_SIZE
    group_length = queries.shape[1] // (kv_heads * HEAD_SIZE)
    seq_count = lax.axis_size("seq")
    section_index = lax.axis_index("section")
    seq_index = lax.axis_index("seq")
    position = section_index * seq_count + seq_index
    first_token = position * tokens
    first_pooled = position * pooled_rows
    pooled_query_rows = pool_rows(queries, query_pooling_weight)
    pooled_key_rows = pool_rows(keys, key_pooling_weight)
    pooled_value_rows = pool_rows(values, value_pooling_weight)
    reach_count = -(-(WINDOW_LENGTH - 1) // tokens)
    older_keys = []
    older_values = []
    carried_query = jnp.zeros((1, queries.shape[1]), jnp.bfloat16)
    for offset in range(reach_count, 0, -1):
        arrived = passed_along((keys, values, pooled_query_rows[-1:]), ("section", "seq"), offset)
        older_keys.append(arrived[0])
        older_values.append(arrived[1])
        if offset == 1:
            carried_query = arrived[2]
    keys_all = jnp.concatenate(older_keys + [keys], axis=0)
    values_all = jnp.concatenate(older_values + [values], axis=0)
    fine_part = window_attention(queries, keys_all, values_all, first_token, reach_count)
    shifted_q = jnp.concatenate([carried_query, pooled_query_rows[:-1]], axis=0)
    shifted_pos = first_pooled - 1 + jnp.arange(pooled_rows)
    query_sets = ((shifted_q, shifted_pos),)
    initial = (empty_state(pooled_rows, kv_heads, group_length),)
    states = fold_blocks(
        initial,
        (
            lax.all_gather(pooled_key_rows, ("section", "seq"), axis=0, tiled=True),
            lax.all_gather(pooled_value_rows, ("section", "seq"), axis=0, tiled=True),
        ),
        query_sets,
        same_position,
    )
    coarse_part = finish_state(states[0])
    expanded_rows = (coarse_part[:, None, :] * up_weight[None]).reshape(tokens, -1)
    combined = fine_part + expanded_rows
    squares = lax.psum(jnp.sum(combined * combined, axis=1), "head")
    scaled = combined * lax.rsqrt(squares / D + 1e-05)[:, None] * out_gain[None]
    return scaled.astype(jnp.bfloat16)


def solution(mesh):
    return jax.shard_map(
        per_device,
        mesh=mesh,
        in_specs=(
            P(("section", "seq"), "head"),
            P(("section", "seq"), "head"),
            P(("section", "seq"), "head"),
            P(None, "head"),
            P(None, "head"),
            P(None, "head"),
            P(None, "head"),
            P("head"),
        ),
        out_specs=P(("section", "seq"), "head"),
        check_vma=False,
    )
```

profile of v0, /device:TPU:31, one launch (start us, length us, event | category | flops | bytes accessed | tf_op | source)
XLA Modules:
  0.0 377.8 jit_solution(16259138230272244509)
XLA Ops:
  14.1 3.4 collective-permute-start.3
  17.6 4.0 %collective-permute-start.2 = (bf16[256,512]{0,1:T(8,128)(2,1)}, bf16[256,512]{0,1:T(8,128)(2,1)}, u32[]{:S(2)}, u32[]{:S(2)}) collective-permute-start(bf16[256,512]{0,1:T(8,128)(2,1)} %copy.33), channel_id=1, source_target_pairs={{0,4},{2,6},{4,8},{6,10},{8,12},{10,14},{12,16},{14,18},{16,20},{1... | collective-permute-start | bytes 786440 | tf_op jit(solution)/shard_map/ppermute | solution.py:15
  32.2 4.5 %collective-permute-start.4 = (bf16[1,2048]{1,0:T(2,128)(2,1)S(1)}, bf16[1,2048]{1,0:T(2,128)(2,1)S(1)}, u32[]{:S(2)}, u32[]{:S(2)}) collective-permute-start(bf16[1,2048]{1,0:T(2,128)(2,1)S(1)} %slice.8), channel_id=1, source_target_pairs={{0,2},{2,4},{4,6},{6,8},{8,10},{10,12},{12,14},{14,16},{16,18},{18... | collective-permute-start | bytes 12296 | tf_op jit(solution)/shard_map/ppermute | solution.py:15
  38.5 5.5 %collective-permute-done.4 = bf16[1,2048]{1,0:T(2,128)(2,1)S(1)} collective-permute-done((bf16[1,2048]{1,0:T(2,128)(2,1)S(1)}, bf16[1,2048]{1,0:T(2,128)(2,1)S(1)}, u32[]{:S(2)}, u32[]{:S(2)}) %collective-permute-start.4) | collective-permute-done | bytes 4128 | tf_op jit(solution)/shard_map/ppermute | solution.py:15
  50.9 4.6 %copy-done.1 = f32[4,768,256,4]{2,1,3,0:T(8,128)} copy-done((f32[4,768,256,4]{2,1,3,0:T(8,128)}, f32[4,768,256,4]{2,1,3,0:T(8,128)S(1)}, u32[]{:S(2)}) %copy-start.1) | copy-done | bytes 12582936
  58.0 86.9 %all-gather.3.cloned.1.call-done = bf16[8192,512]{1,0:T(8,128)(2,1)} async-done(((bf16[64,512]{1,0:T(8,128)(2,1)}), bf16[8192,512]{1,0:T(8,128)(2,1)}) %all-gather.3.cloned.1.call-update) | async-done | bytes 8388624 | tf_op jit(solution)/shard_map/all_gather | solution.py:169
  144.9 11.9 %copy.39 = bf16[8192,512]{0,1:T(8,128)(2,1)} copy(bf16[8192,512]{1,0:T(8,128)(2,1)} %all-gather.3.cloned.1.call-done) | data formatting | bytes 16777216
  156.9 112.7 %all-gather.5.cloned.1.call-done = bf16[8192,512]{1,0:T(8,128)(2,1)} async-done(((bf16[64,512]{1,0:T(8,128)(2,1)}), bf16[8192,512]{1,0:T(8,128)(2,1)}) %all-gather.5.cloned.1.call-update) | async-done | bytes 8388624 | tf_op jit(solution)/shard_map/all_gather | solution.py:170
  269.5 11.4 %copy.40 = bf16[8192,512]{0,1:T(8,128)(2,1)} copy(bf16[8192,512]{1,0:T(8,128)(2,1)} %all-gather.5.cloned.1.call-done) | data formatting | bytes 16777216
  281.8 57.2 %while.19 = (s32[]{:T(128)}, f32[4,4,64]{2,1,0:T(4,128)S(1)}, f32[4,4,64]{2,1,0:T(4,128)S(1)}, f32[4,4,64,128]{3,2,1,0:T(8,128)}, s32[]{:T(128)}, /*index=5*/bf1...) while((s32[]{:T(128)}, f32[4,4,64]{2,1,0:T(4,128)S(1)}, ...), condition=%wide.region_12.13_spmd.clone, body=%wide.region_6.12_spmd.clone.sunk | while | flops 1097213952 | bytes 48584040 | solution.py:112
  283.8 12.2 %conditional.3 = ((f32[4,4,64]{2,1,0:T(4,128)S(1)}, f32[4,4,64]{2,1,0:T(4,128)S(1)}, f32[4,4,64,128]{3,2,1,0:T(8,128)})) conditional(s32[]{:T(128)} %convert_element_type.74, (f32[4,4,64]{2,1,0:T(4,128)S(1)}, f32[4,4,64]{2,1,0:T(4,128)S(1)}, f32[4,4,64,128]{3,2,1,0:T(8,128)}) %tuple.66, (s32[2048]{0:T(1024)S(1)}, s32[]{:T(128)}, s32[]{:T(128)}, ...), branch_computations={%region_8.8_spmd, %region_9.11_spmd} | conditional | flops 1097209856 | bytes 48575336 | solution.py:87
  284.0 4.0 %constant_dynamic-slice_fusion = (bf16[2048,512]{0,1:T(8,128)(2,1)}, bf16[2048,512]{0,1:T(8,128)(2,1)S(1)}) fusion(bf16[8192,512]{0,1:T(8,128)(2,1)} %get-tuple-element.285, s32[]{:T(128)S(6)} %select_n.28, bf16[8192,512]{0,1:T(8,128)(2,1)} %get-tuple-element.280), kind=kLoop, calls=%fused_computation.15 | loop fusion | bytes 8388612 | tf_op jit(solution)/shard_map/while/body/eval_jaxpr/dynamic_slice | solution.py:101
  292.0 4.0 %fusion.8 = f32[4,4,64,128]{3,2,1,0:T(8,128)} fusion(bf16[2048,4,128,1]{0,2,3,1:T(8,128)(2,1)S(1)} %bitcast.56, f32[4,2048,64,4]{1,2,3,0:T(8,128)S(1)} %get-tuple-element.362, f32[4,4,64]{2,1,0:T(4,128)S(1)} %get-tuple-element.359, pred[64,2048]{1,0:T(8,128)(4,1)S(1)} %broadcast_compare_fusion, f32[4,4,64,128]{3,2,1,0:T(8,128)} %get-tuple-element.284, ...), kind=kOutput, calls=%fused_computation.8 | convolution fusion | flops 545521664 | bytes 11673600 | tf_op jit(solution)/shard_map/while/body/eval_jaxpr/cond/branch_1_fun/hgqk,khd->hgqd/dot_general | solution.py:73
  298.1 12.2 %conditional.3 = ((f32[4,4,64]{2,1,0:T(4,128)S(1)}, f32[4,4,64]{2,1,0:T(4,128)S(1)}, f32[4,4,64,128]{3,2,1,0:T(8,128)})) conditional(s32[]{:T(128)} %convert_element_type.74, (f32[4,4,64]{2,1,0:T(4,128)S(1)}, f32[4,4,64]{2,1,0:T(4,128)S(1)}, f32[4,4,64,128]{3,2,1,0:T(8,128)}) %tuple.66, (s32[2048]{0:T(1024)S(1)}, s32[]{:T(128)}, s32[]{:T(128)}, ...), branch_computations={%region_8.8_spmd, %region_9.11_spmd} | conditional | flops 1097209856 | bytes 48575336 | solution.py:87
  298.3 4.0 %constant_dynamic-slice_fusion = (bf16[2048,512]{0,1:T(8,128)(2,1)}, bf16[2048,512]{0,1:T(8,128)(2,1)S(1)}) fusion(bf16[8192,512]{0,1:T(8,128)(2,1)} %get-tuple-element.285, s32[]{:T(128)S(6)} %select_n.28, bf16[8192,512]{0,1:T(8,128)(2,1)} %get-tuple-element.280), kind=kLoop, calls=%fused_computation.15 | loop fusion | bytes 8388612 | tf_op jit(solution)/shard_map/while/body/eval_jaxpr/dynamic_slice | solution.py:101
  306.3 4.0 %fusion.8 = f32[4,4,64,128]{3,2,1,0:T(8,128)} fusion(bf16[2048,4,128,1]{0,2,3,1:T(8,128)(2,1)S(1)} %bitcast.56, f32[4,2048,64,4]{1,2,3,0:T(8,128)S(1)} %get-tuple-element.362, f32[4,4,64]{2,1,0:T(4,128)S(1)} %get-tuple-element.359, pred[64,2048]{1,0:T(8,128)(4,1)S(1)} %broadcast_compare_fusion, f32[4,4,64,128]{3,2,1,0:T(8,128)} %get-tuple-element.284, ...), kind=kOutput, calls=%fused_computation.8 | convolution fusion | flops 545521664 | bytes 11673600 | tf_op jit(solution)/shard_map/while/body/eval_jaxpr/cond/branch_1_fun/hgqk,khd->hgqd/dot_general | solution.py:73
  312.4 12.2 %conditional.3 = ((f32[4,4,64]{2,1,0:T(4,128)S(1)}, f32[4,4,64]{2,1,0:T(4,128)S(1)}, f32[4,4,64,128]{3,2,1,0:T(8,128)})) conditional(s32[]{:T(128)} %convert_element_type.74, (f32[4,4,64]{2,1,0:T(4,128)S(1)}, f32[4,4,64]{2,1,0:T(4,128)S(1)}, f32[4,4,64,128]{3,2,1,0:T(8,128)}) %tuple.66, (s32[2048]{0:T(1024)S(1)}, s32[]{:T(128)}, s32[]{:T(128)}, ...), branch_computations={%region_8.8_spmd, %region_9.11_spmd} | conditional | flops 1097209856 | bytes 48575336 | solution.py:87
  312.6 4.0 %constant_dynamic-slice_fusion = (bf16[2048,512]{0,1:T(8,128)(2,1)}, bf16[2048,512]{0,1:T(8,128)(2,1)S(1)}) fusion(bf16[8192,512]{0,1:T(8,128)(2,1)} %get-tuple-element.285, s32[]{:T(128)S(6)} %select_n.28, bf16[8192,512]{0,1:T(8,128)(2,1)} %get-tuple-element.280), kind=kLoop, calls=%fused_computation.15 | loop fusion | bytes 8388612 | tf_op jit(solution)/shard_map/while/body/eval_jaxpr/dynamic_slice | solution.py:101
  320.6 4.0 %fusion.8 = f32[4,4,64,128]{3,2,1,0:T(8,128)} fusion(bf16[2048,4,128,1]{0,2,3,1:T(8,128)(2,1)S(1)} %bitcast.56, f32[4,2048,64,4]{1,2,3,0:T(8,128)S(1)} %get-tuple-element.362, f32[4,4,64]{2,1,0:T(4,128)S(1)} %get-tuple-element.359, pred[64,2048]{1,0:T(8,128)(4,1)S(1)} %broadcast_compare_fusion, f32[4,4,64,128]{3,2,1,0:T(8,128)} %get-tuple-element.284, ...), kind=kOutput, calls=%fused_computation.8 | convolution fusion | flops 545521664 | bytes 11673600 | tf_op jit(solution)/shard_map/while/body/eval_jaxpr/cond/branch_1_fun/hgqk,khd->hgqd/dot_general | solution.py:73
  326.7 12.2 %conditional.3 = ((f32[4,4,64]{2,1,0:T(4,128)S(1)}, f32[4,4,64]{2,1,0:T(4,128)S(1)}, f32[4,4,64,128]{3,2,1,0:T(8,128)})) conditional(s32[]{:T(128)} %convert_element_type.74, (f32[4,4,64]{2,1,0:T(4,128)S(1)}, f32[4,4,64]{2,1,0:T(4,128)S(1)}, f32[4,4,64,128]{3,2,1,0:T(8,128)}) %tuple.66, (s32[2048]{0:T(1024)S(1)}, s32[]{:T(128)}, s32[]{:T(128)}, ...), branch_computations={%region_8.8_spmd, %region_9.11_spmd} | conditional | flops 1097209856 | bytes 48575336 | solution.py:87
  326.9 4.0 %constant_dynamic-slice_fusion = (bf16[2048,512]{0,1:T(8,128)(2,1)}, bf16[2048,512]{0,1:T(8,128)(2,1)S(1)}) fusion(bf16[8192,512]{0,1:T(8,128)(2,1)} %get-tuple-element.285, s32[]{:T(128)S(6)} %select_n.28, bf16[8192,512]{0,1:T(8,128)(2,1)} %get-tuple-element.280), kind=kLoop, calls=%fused_computation.15 | loop fusion | bytes 8388612 | tf_op jit(solution)/shard_map/while/body/eval_jaxpr/dynamic_slice | solution.py:101
  334.9 4.0 %fusion.8 = f32[4,4,64,128]{3,2,1,0:T(8,128)} fusion(bf16[2048,4,128,1]{0,2,3,1:T(8,128)(2,1)S(1)} %bitcast.56, f32[4,2048,64,4]{1,2,3,0:T(8,128)S(1)} %get-tuple-element.362, f32[4,4,64]{2,1,0:T(4,128)S(1)} %get-tuple-element.359, pred[64,2048]{1,0:T(8,128)(4,1)S(1)} %broadcast_compare_fusion, f32[4,4,64,128]{3,2,1,0:T(8,128)} %get-tuple-element.284, ...), kind=kOutput, calls=%fused_computation.8 | convolution fusion | flops 545521664 | bytes 11673600 | tf_op jit(solution)/shard_map/while/body/eval_jaxpr/cond/branch_1_fun/hgqk,khd->hgqd/dot_general | solution.py:73
  348.9 10.0 %multiply_reduce_fusion = (f32[256]{0:T(256)S(1)}, f32[256,4,4,128]{0,3,2,1:T(8,128)}) fusion(f32[256,4,4,128]{0,3,2,1:T(8,128)} %copy.43, f32[256,4,4]{0,2,1:T(4,128)S(1)} %bitcast.61, bf16[768,4,128,1]{0,2,3,1:T(8,128)(2,1)S(1)} %bitcast.60, f32[4,768,256,4]{2,1,3,0:T(8,128)} %copy-done.1, f32[4,4,256]{2,1,0:T(4,128)S(1)} %get-tuple-element.367, ...), kind=kOutput, calls=%fused_computation.31 | convolution fusion | flops 819986176 | bytes 17794048 | tf_op jit(solution)/shard_map/hgqk,khd->qhgd/dot_general | solution.py:44
  361.8 6.3 %psum.7 = f32[256]{0:T(256)S(1)} all-reduce(f32[256]{0:T(256)S(1)} %get-tuple-element.369), channel_id=1, replica_groups=mesh['section'=4,'seq'=32,'head'=2] {'head'}, use_global_device_ids=true, to_apply=%region_14.15 | all-reduce | flops 256 | bytes 2048 | tf_op jit(solution)/shard_map/psum | solution.py:178
  (107 shorter events, 65.0 us)
Async XLA Ops:
  6.5 30.5 %copy-start.3 = (bf16[256,2048]{1,0:T(8,128)(2,1)S(1)}, bf16[256,2048]{1,0:T(8,128)(2,1)}, u32[]{:S(2)}) copy-start(bf16[256,2048]{1,0:T(8,128)(2,1)} %param.12) | copy-start | bytes 3145732
  6.5 23.5 %copy-start.6 = (f32[4,2048]{1,0:T(4,128)S(1)}, f32[4,2048]{1,0:T(4,128)}, u32[]{:S(2)}) copy-start(f32[4,2048]{1,0:T(4,128)} %param.15) | copy-start | bytes 98308
  6.5 138.4 %all-gather.3.cloned.1.call-start = ((), (), s32[]{:S(2)}) async-start(), calls=%async_computation | async-start | bytes 8454144 | tf_op jit(solution)/shard_map/all_gather | solution.py:169
  9.5 260.1 %all-gather.5.cloned.1.call-start = ((), (), s32[]{:S(2)}) async-start(), calls=%async_computation.1 | async-start | bytes 8454144 | tf_op jit(solution)/shard_map/all_gather | solution.py:170
  14.1 33.3 %collective-permute-start.3 = (bf16[256,512]{0,1:T(8,128)(2,1)}, bf16[256,512]{0,1:T(8,128)(2,1)}, u32[]{:S(2)}, u32[]{:S(2)}) collective-permute-start(bf16[256,512]{0,1:T(8,128)(2,1)} %copy.33), channel_id=1, source_target_pairs={{0,2},{2,4},{4,6},{6,8},{8,10},{10,12},{12,14},{14,16},{16,18},{18... | collective-permute-start | bytes 786440 | tf_op jit(solution)/shard_map/ppermute | solution.py:15
  17.6 29.9 %collective-permute-start.2 = (bf16[256,512]{0,1:T(8,128)(2,1)}, bf16[256,512]{0,1:T(8,128)(2,1)}, u32[]{:S(2)}, u32[]{:S(2)}) collective-permute-start(bf16[256,512]{0,1:T(8,128)(2,1)} %copy.33), channel_id=1, source_target_pairs={{0,4},{2,6},{4,8},{6,10},{8,12},{10,14},{12,16},{14,18},{16,20},{1... | collective-permute-start | bytes 786440 | tf_op jit(solution)/shard_map/ppermute | solution.py:15
  21.6 23.5 %collective-permute-start.1 = (bf16[256,512]{1,0:T(8,128)(2,1)}, bf16[256,512]{1,0:T(8,128)(2,1)}, u32[]{:S(2)}, u32[]{:S(2)}) collective-permute-start(bf16[256,512]{1,0:T(8,128)(2,1)} %param.14), channel_id=1, source_target_pairs={{0,2},{2,4},{4,6},{6,8},{8,10},{10,12},{12,14},{14,16},{16,18},{18... | collective-permute-start | bytes 786440 | tf_op jit(solution)/shard_map/ppermute | solution.py:15
  25.1 20.0 %collective-permute-start = (bf16[256,512]{1,0:T(8,128)(2,1)}, bf16[256,512]{1,0:T(8,128)(2,1)}, u32[]{:S(2)}, u32[]{:S(2)}) collective-permute-start(bf16[256,512]{1,0:T(8,128)(2,1)} %param.14), channel_id=1, source_target_pairs={{0,4},{2,6},{4,8},{6,10},{8,12},{10,14},{12,16},{14,18},{16,20},{1... | collective-permute-start | bytes 786440 | tf_op jit(solution)/shard_map/ppermute | solution.py:15
  31.5 0.7 copy-start.4
  32.2 11.8 %collective-permute-start.4 = (bf16[1,2048]{1,0:T(2,128)(2,1)S(1)}, bf16[1,2048]{1,0:T(2,128)(2,1)S(1)}, u32[]{:S(2)}, u32[]{:S(2)}) collective-permute-start(bf16[1,2048]{1,0:T(2,128)(2,1)S(1)} %slice.8), channel_id=1, source_target_pairs={{0,2},{2,4},{4,6},{6,8},{8,10},{10,12},{12,14},{14,16},{16,18},{18... | collective-permute-start | bytes 12296 | tf_op jit(solution)/shard_map/ppermute | solution.py:15
  50.9 4.6 %copy-start.1 = (f32[4,768,256,4]{2,1,3,0:T(8,128)}, f32[4,768,256,4]{2,1,3,0:T(8,128)S(1)}, u32[]{:S(2)}) copy-start(f32[4,768,256,4]{2,1,3,0:T(8,128)S(1)} %get-tuple-element.368) | copy-start | bytes 37748740
  281.8 59.0 %copy-start.7 = (f32[4,2048]{1,0:T(4,128)S(1)}, f32[4,2048]{1,0:T(4,128)}, u32[]{:S(2)}) copy-start(f32[4,2048]{1,0:T(4,128)} %param.18) | copy-start | bytes 98308
  289.8 2.2 copy-start
  304.1 2.2 copy-start
  318.4 2.2 copy-start
  332.7 2.2 copy-start
  341.4 7.5 %copy-start.5 = (bf16[768,512]{0,1:T(8,128)(2,1)S(1)}, bf16[768,512]{0,1:T(8,128)(2,1)}, u32[]{:S(2)}) copy-start(bf16[768,512]{0,1:T(8,128)(2,1)} %copy.32) | copy-start | bytes 2359300
  348.9 19.3 %copy-start.2 = (f32[256,2048]{1,0:T(8,128)S(1)}, f32[256,2048]{1,0:T(8,128)}, u32[]{:S(2)}) copy-start(f32[256,2048]{1,0:T(8,128)} %mul.138) | copy-start | bytes 6291460
  348.9 19.3 %copy-start.8 = (f32[2048]{0:T(1024)S(1)}, f32[2048]{0:T(1024)}, u32[]{:S(2)}) copy-start(f32[2048]{0:T(1024)} %param.19) | copy-start | bytes 24580
Sparse Core Ops, SparseCore 0:
  11.0 133.9 all-gather.2
  148.6 120.8 all-gather.4
where the time goes:
time: 381 us; the launch traced here: 378 us
  waiting for transfers between devices  205 us (54%)
  local copies, waits for them, and re-layouts  65.1 us (17%)
  matrix products  34.6 us (9%)
  other arithmetic  28.7 us (8%)
  starting transfers between devices  18.7 us (5%)
  between operations  13.6 us (4%)
  blocking collectives  6.33 us (2%)
  loops' own time  5.78 us (2%)
    all_gather x1, waiting for transfers between devices, per_device(): lax.all_gather(pooled_value_rows, ('section', 'seq'), axis=0, tiled=True)  113 us
    all_gather x1, waiting for transfers between devices, per_device(): lax.all_gather(pooled_key_rows, ('section', 'seq'), axis=0, tiled=True)  86.9 us
    unnamed x19, local copies, waits for them, and re-layouts  30.3 us
    ppermute x5, starting transfers between devices, passed_along(): lax.ppermute(value, axis, [(source, source + steps) for source in range(i...  18.6 us
    dynamic_slice x4, local copies, waits for them, and re-layouts, one_block(): lax.dynamic_slice_in_dim(piece_values, starting_row, block_rows, 0)  16.2 us
    dot_general x4, matrix products, coarse_update(): jnp.einsum('hgqk,khd->hgqd', weights.astype(jnp.bfloat16), shaped_v, pref...  16 us
    dot_general x1, matrix products, window_attention(): jnp.einsum('hgqk,khd->qhgd', weights.astype(jnp.bfloat16), shaped_v, pref...  9.99 us
    reduce_sum x4, other arithmetic, coarse_update(): running_sum = running_sum * rescale + jnp.sum(weights, axis=-1)  8.71 us
  transfers between devices with their start and end apart: 7, of which 3 were waited for; matrix products, arithmetic and copies ran while one was open for 8% of the time, Pallas kernels for 0%

commit v1 on v0

v1 whole, which is shorter than its diff:
```python
import functools

import jax
import jax.numpy as jnp
from jax import lax
from jax.experimental import pallas as pl
from jax.experimental.pallas import tpu as pltpu
from jax.sharding import PartitionSpec as P

MESH = pl.DeviceIdType.MESH
HEAD = 128
POOL = 4
WINDOW = 512
NX = 4
QUERY_ROWS = 16
SCALE = 1.4426950408889634 * HEAD ** -0.5
MASKED = -1e30
FLOOR = -1e29
BF = jnp.bfloat16
F32 = jnp.float32


def split_pair(value):
    high = value.astype(BF)
    low = (value - high.astype(F32)).astype(BF)
    return high, low


def dot(a, b):
    return lax.dot_general(a, b, (((1,), (0,)), ((), ())), preferred_element_type=F32)


def dot_t(a, b):
    return lax.dot_general(a, b, (((1,), (1,)), ((), ())), preferred_element_type=F32)


def iota(shape, dim):
    return lax.broadcasted_iota(jnp.int32, shape, dim)


def one_hot_groups(rows, columns, period, offset):
    r = iota((rows, columns), 0)
    c = lax.rem(iota((rows, columns), 1), period)
    first = c - offset - POOL * r
    return jnp.where((first >= 0) & (first < POOL), 1.0, 0.0).astype(BF)


def weighted_pair(rows, weights8):
    count, columns = rows.shape
    product = (rows.astype(F32).reshape(count // 8, 8, columns) * weights8[None]).reshape(count, columns)
    high, low = split_pair(product)
    return jnp.concatenate([high, low], axis=0)


def kernel(ny, nz, q_ref, k_ref, v_ref, qw_ref, kw_ref, vw_ref, up_ref, gain_ref, out_ref,
           ga, gb, hk1, hv1, hk2, hv2, hq, qall, qhl, acc, mst, osend, orecv, ssend, srecv,
           fine, bias, ssq, ssq_in, send_sem, recv_sem):
    tokens = q_ref.shape[0]
    rows = tokens // POOL
    y = lax.axis_index("section")
    s = lax.axis_index("seq")
    h = lax.axis_index("head")
    ns = NX * nz
    z = lax.div(s, NX)
    x = lax.rem(s, NX)
    position = y * ns + s
    plus_steps = (nz - 1) // 2
    minus_steps = nz - 1 - plus_steps

    def wrap(value, size):
        return lax.rem(value + 2 * size, size)

    def at(zz, xx):
        return (y, zz * NX + xx, h)

    def at_position(pp):
        return (lax.div(pp, ns), lax.rem(pp, ns), h)

    x_next, x_prev, x_far = wrap(x + 1, NX), wrap(x - 1, NX), wrap(x + 2, NX)
    right, left = at(z, x_next), at(z, x_prev)
    above, below = at(wrap(z + 1, nz), x), at(wrap(z - 1, nz), x)
    following = at_position(lax.rem(position + 1, ny * ns))
    preceding = at_position(lax.rem(position + ny * ns - 1, ny * ns))
    partner = (y, s, 1 - h)

    barrier = pltpu.get_barrier_semaphore()
    peers = [right, left, above, below, following, preceding, partner]
    peers += [(lax.rem(y + step, ny), s, h) for step in range(1, ny)]
    for peer in peers:
        pl.semaphore_signal(barrier, inc=1, device_id=peer, device_id_type=MESH)

    per_wave = 3 + 2 * (nz - 1) + 6
    ax0, az0, bz0, bx0 = 0, 3, 3 + (nz - 1), 3 + 2 * (nz - 1)
    halo0 = 2 * per_wave
    q0 = halo0 + 5
    o0 = q0 + ny
    norm0 = o0 + 2 * ny * 2

    def remote(src, dst, send_index, recv_index, device):
        return pltpu.make_async_remote_copy(
            src_ref=src, dst_ref=dst, send_sem=send_sem.at[send_index],
            recv_sem=recv_sem.at[recv_index], device_id=device, device_id_type=MESH)

    unconditional = []

    def send(ref, index, device, dst=None, key=None):
        copy = remote(ref, ref if dst is None else dst, index if key is None else key, index, device)
        copy.start()
        unconditional.append(copy)

    def arrived(ref, index):
        remote(ref, ref, index, index, left).wait_recv()

    pool_plain = one_hot_groups(rows, 2 * tokens, tokens, 0)
    for wave in range(2):
        for kind in range(2):
            kv = 2 * wave + kind
            columns = slice(kv * HEAD, (kv + 1) * HEAD)
            pooled_k = dot(pool_plain, weighted_pair(k_ref[:, columns], kw_ref[:, columns])).astype(BF)
            pooled_v = dot(pool_plain, weighted_pair(v_ref[:, columns], vw_ref[:, columns])).astype(BF)
            block = jnp.concatenate([pooled_k, pooled_v], axis=1)
            if kind == 0:
                ga[wave, z, x] = block
            else:
                gb[wave, x, z] = block
    pl.semaphore_wait(barrier, len(peers))

    def ax_start(w):
        base = w * per_wave + ax0
        send(ga.at[w, z, x], base + 1, left)
        send(ga.at[w, z, x], base + 0, right)

    def ax_rest(w):
        base = w * per_wave + ax0
        arrived(ga.at[w, z, x_next], base + 1)
        send(ga.at[w, z, x_next], base + 2, left)
        arrived(ga.at[w, z, x_prev], base + 0)
        arrived(ga.at[w, z, x_far], base + 2)

    def z_plus(ref_at, base, d):
        if d > 0:
            arrived(ref_at(wrap(z - d, nz)), base + d - 1)
        if d < plus_steps:
            send(ref_at(wrap(z - d, nz)), base + d, above)

    def z_minus(ref_at, base, d):
        base = base + plus_steps
        if d > 0:
            arrived(ref_at(wrap(z + d, nz)), base + d - 1)
        if d < minus_steps:
            send(ref_at(wrap(z + d, nz)), base + d, below)

    def az(w, d):
        ref_at = lambda zz: ga.at[w, zz]
        if d <= minus_steps:
            z_minus(ref_at, w * per_wave + az0, d)
        if d <= plus_steps:
            z_plus(ref_at, w * per_wave + az0, d)

    def bz(w, d):
        ref_at = lambda zz: gb.at[w, x, zz]
        if d <= minus_steps:
            z_minus(ref_at, w * per_wave + bz0, d)
        if d <= plus_steps:
            z_plus(ref_at, w * per_wave + bz0, d)

    half_rows = nz // 2

    def half_of(w, xx, half):
        return gb.at[w, xx, pl.ds(half * half_rows, half_rows)]

    def bx_start(w, half):
        base = w * per_wave + bx0 + 3 * half
        send(half_of(w, x, half), base + 1, left)
        send(half_of(w, x, half), base + 0, right)

    def bx_relay(w, half):
        base = w * per_wave + bx0 + 3 * half
        arrived(half_of(w, x_next, half), base + 1)
        send(half_of(w, x_next, half), base + 2, left)

    def bx_rest(w, half):
        base = w * per_wave + bx0 + 3 * half
        arrived(half_of(w, x_prev, half), base + 0)
        arrived(half_of(w, x_far, half), base + 2)

    send(q_ref.at[pl.ds(tokens - QUERY_ROWS, QUERY_ROWS)], halo0 + 4, following, hq)
    for w in range(2):
        ax_start(w)
        bz(w, 0)
    send(k_ref, halo0 + 0, following, hk1)
    send(v_ref, halo0 + 1, following, hv1)

    r = iota((tokens, tokens), 0)
    c = iota((tokens, tokens), 1)
    bias[:, 0:tokens] = jnp.where((c > r) & (position >= 2), 0.0, MASKED)
    bias[:, tokens:2 * tokens] = jnp.where((c >= 0) & (position >= 1), 0.0, MASKED)
    bias[:, 2 * tokens:3 * tokens] = jnp.where(c <= r, 0.0, MASKED)

    arrived(hq, halo0 + 4)
    pool_shifted = one_hot_groups(rows, 2 * (tokens + QUERY_ROWS), tokens + QUERY_ROWS, QUERY_ROWS - POOL)
    heads = q_ref.shape[1] // HEAD

    def pool_head(n, carry):
        columns = pl.ds(pl.multiple_of(n * HEAD, HEAD), HEAD)
        joined = jnp.concatenate([hq[:, columns], q_ref[:, columns]], axis=0)
        pooled = dot(pool_shifted, weighted_pair(joined, qw_ref[:, columns])).astype(BF)
        qall[y, :, columns] = pooled
        return carry

    lax.fori_loop(0, heads, pool_head, 0)

    def prepare(t):
        def one(n, carry):
            columns = pl.ds(pl.multiple_of(n * HEAD, HEAD), HEAD)
            high, low = split_pair(qall[t, :, columns].astype(F32) * SCALE)
            group = pl.ds(pl.multiple_of(lax.rem(n, 4) * rows, rows), rows)
            qhl[t, lax.div(n, 4), group, :] = jnp.concatenate([high, low], axis=1)
            return carry

        lax.fori_loop(0, heads, one, 0)

    ax_rest(0)
    az(0, 0)
    bz(0, 1)
    ax_rest(1)
    az(1, 0)
    bz(1, 1)
    for lower in range(ny - 1):
        @pl.when(y > lower)
        def _():
            remote(qall.at[y], qall.at[y], q0 + lower, q0 + y, (lower, s, h)).start()
    prepare(y)
    for d in range(2, minus_steps + 1):
        bz(0, d)
        bz(1, d)
    for t in range(1, ny):
        @pl.when(t > y)
        def _():
            arrived(qall.at[t], q0 + t)
            prepare(t)
    for half in range(2):
        bx_start(0, half)

    def coarse(kv, load, key_position, first):
        def body(t, carry):
            keys, values = load()
            scores = dot_t(qhl[t, kv], jnp.concatenate([keys, keys], axis=1))
            limit = rows * s + lax.rem(iota((4 * rows, 1), 0), rows)
            limit = jnp.where(t > y, jnp.int32(1 << 30), limit)
            scores = jnp.where(key_position < limit, scores, MASKED)
            newest = jnp.max(scores, axis=1, keepdims=True)
            if first:
                newest = jnp.maximum(newest, FLOOR)
            else:
                before = mst[kv, t]
                newest = jnp.maximum(before, newest)
            if first:
                top = newest
                mst[kv, t] = jnp.broadcast_to(newest, (4 * rows, HEAD))
            else:
                top = newest[:, :1]
                mst[kv, t] = newest
            weights = jnp.exp2(scores - top).astype(BF)
            blended = dot(weights, jnp.concatenate([values, jnp.ones_like(values)], axis=1))
            if first:
                acc[kv, t] = blended
            else:
                shrink = jnp.exp2(before - newest)
                acc[kv, t] = acc[kv, t] * jnp.concatenate([shrink, shrink], axis=1) + blended
            return carry

        lax.fori_loop(y, ny, body, 0)

    def coarse_a(w, z_one, z_two, first=False):
        def load():
            count = NX * rows
            both = jnp.concatenate([ga[w, z_one].reshape(count, 2 * HEAD), ga[w, z_two].reshape(count, 2 * HEAD)], axis=0)
            return both[:, :HEAD], both[:, HEAD:]

        count = NX * rows
        index = iota((1, 2 * count), 1)
        place = jnp.where(index < count, z_one * count + index, z_two * count + index - count)
        coarse(2 * w, load, place, first)

    def coarse_b(w, half, first=False):
        def load():
            whole = gb[w, :, half * half_rows:(half + 1) * half_rows].reshape(NX * half_rows * rows, 2 * HEAD)
            return whole[:, :HEAD], whole[:, HEAD:]

        index = iota((1, NX * half_rows * rows), 1)
        xx = lax.div(index, half_rows * rows)
        zz = lax.rem(lax.div(index, rows), half_rows) + half * half_rows
        place = (zz * NX + xx) * rows + lax.rem(index, rows)
        coarse(2 * w + 1, load, place, first)

    def finish(w, kind):
        kv = 2 * w + kind
        lane = iota((rows, HEAD), 1)
        for t in range(1, ny):
            @pl.when(t > y)
            def _():
                stats = jnp.zeros((rows, HEAD), F32) if kind == 0 else ssend[w, t]
                for g in range(4):
                    part = slice(g * rows, (g + 1) * rows)
                    total = acc[kv, t, part, HEAD:]
                    column = (kind * 4 + g) * HEAD
                    osend[w, t, :, column:column + HEAD] = (acc[kv, t, part, :HEAD] / total).astype(BF)
                    stats = jnp.where(lane == kind * 4 + g, mst[kv, t, part] + jnp.log2(total), stats)
                ssend[w, t] = stats

    def partial_copies(w, t):
        base = o0 + w * 2 * ny
        return (
            remote(osend.at[w, t], orecv.at[w, y], base + 2 * t, base + 2 * y, (t, s, h)),
            remote(ssend.at[w, t], srecv.at[w, y], base + 2 * t + 1, base + 2 * y + 1, (t, s, h)),
        )

    def send_partials(w):
        for t in range(1, ny):
            @pl.when(t > y)
            def _():
                for copy in partial_copies(w, t):
                    copy.start()

    def z_up(d):
        return wrap(z + d, nz)

    az(0, 1)
    for half in range(2):
        bx_start(1, half)
    az(1, 1)
    for half in range(2):
        bx_relay(0, half)
    coarse_a(0, z, z_up(-1), True)
    az(0, 2)
    arrived(hk1, halo0 + 0)
    send(hk1, halo0 + 2, following, hk2)
    arrived(hv1, halo0 + 1)
    send(hv1, halo0 + 3, following, hv2)
    coarse_a(1, z, z_up(-1), True)
    az(1, 2)
    coarse_a(0, z_up(1), z_up(-2))
    az(0, 3)
    bx_rest(0, 0)
    bx_rest(0, 1)
    for half in range(2):
        bx_relay(1, half)
    coarse_b(0, 0, True)
    az(1, 3)
    coarse_b(0, 1)
    coarse_a(0, z_up(2), z_up(-3))
    az(0, 4)
    coarse_a(1, z_up(1), z_up(-2))
    coarse_a(0, z_up(3), z_up(4))
    finish(0, 0)
    finish(0, 1)
    send_partials(0)
    bx_rest(1, 0)
    coarse_b(1, 0, True)
    bx_rest(1, 1)
    coarse_b(1, 1)
    coarse_a(1, z_up(2), z_up(-3))
    az(1, 4)
    coarse_a(1, z_up(3), z_up(4))
    finish(1, 0)
    finish(1, 1)
    send_partials(1)

    arrived(hk2, halo0 + 2)
    arrived(hv2, halo0 + 3)

    def window_head(n, carry):
        columns = pl.ds(pl.multiple_of(n * HEAD, HEAD), HEAD)
        kv_columns = pl.ds(pl.multiple_of(lax.div(n, 4) * HEAD, HEAD), HEAD)
        high, low = split_pair(q_ref[:, columns].astype(F32) * SCALE)
        keys = jnp.concatenate([hk2[:, kv_columns], hk1[:, kv_columns], k_ref[:, kv_columns]], axis=0)
        values = jnp.concatenate([hv2[:, kv_columns], hv1[:, kv_columns], v_ref[:, kv_columns]], axis=0)
        scores = dot_t(jnp.concatenate([high, low], axis=1), jnp.concatenate([keys, keys], axis=1)) + bias[...]
        weights = jnp.exp2(scores - jnp.max(scores, axis=1, keepdims=True)).astype(BF)
        blended = dot(weights, jnp.concatenate([values, jnp.ones_like(values)], axis=1))
        fine[:, columns] = blended[:, :HEAD] / blended[:, HEAD:]
        return carry

    lax.fori_loop(0, heads, window_head, 0)

    for w in range(2):
        for src in range(ny - 1):
            @pl.when(src < y)
            def _():
                base = o0 + w * 2 * ny
                arrived(orecv.at[w, src], base + 2 * src)
                arrived(srecv.at[w, src], base + 2 * src + 1)

    expand = jnp.where(
        lax.rem(iota((tokens, 2 * rows), 1), rows) == lax.div(iota((tokens, 2 * rows), 0), POOL), 1.0, 0.0).astype(BF)
    squares = jnp.zeros((tokens, HEAD), F32)
    for w in range(2):
        for kind in range(2):
            kv = 2 * w + kind
            for g in range(4):
                part = slice(g * rows, (g + 1) * rows)
                lane = kind * 4 + g
                state = (mst[kv, y, part], acc[kv, y, part, :HEAD], acc[kv, y, part, HEAD:])

                def join(src, state):
                    top, number, total = state
                    other = jnp.broadcast_to(srecv[w, src][:, lane:lane + 1], (rows, HEAD))
                    newest = jnp.maximum(top, other)
                    mine, theirs = jnp.exp2(top - newest), jnp.exp2(other - newest)
                    blended = orecv[w, src, :, lane * HEAD:(lane + 1) * HEAD].astype(F32)
                    return newest, number * mine + blended * theirs, total * mine + theirs

                top, number, total = lax.fori_loop(0, y, join, state)
                coarse_out = jnp.where(total > 0.0, number / jnp.where(total > 0.0, total, 1.0), 0.0)
                high, low = split_pair(coarse_out)
                spread = dot(expand, jnp.concatenate([high, low], axis=0))
                columns = slice((kv * 4 + g) * HEAD, (kv * 4 + g + 1) * HEAD)
                lifted = (spread.reshape(tokens // 8, 8, HEAD) * up_ref[:, columns][None]).reshape(tokens, HEAD)
                combined = fine[:, columns] + lifted
                fine[:, columns] = combined
                squares = squares + combined * combined
    ssq[...] = squares
    send(ssq, norm0, partner, ssq_in)
    arrived(ssq_in, norm0)
    mean = jnp.sum(squares + ssq_in[...], axis=1, keepdims=True) / (2.0 * q_ref.shape[1])
    factor = jnp.broadcast_to(lax.rsqrt(mean + 1e-05), (tokens, HEAD))
    for n in range(heads):
        columns = slice(n * HEAD, (n + 1) * HEAD)
        out_ref[:, columns] = (fine[:, columns] * factor * gain_ref[:, columns]).astype(BF)

    for copy in unconditional:
        copy.wait_send()
    for lower in range(ny - 1):
        @pl.when(y > lower)
        def _():
            remote(qall.at[y], qall.at[y], q0 + lower, q0 + y, (lower, s, h)).wait_send()
    for w in range(2):
        for t in range(1, ny):
            @pl.when(t > y)
            def _():
                for copy in partial_copies(w, t):
                    copy.wait_send()


def per_device(ny, ns, queries, keys, values, qw, kw, vw, up, gain):
    nz = ns // NX
    tokens, width = queries.shape
    kv_width = keys.shape[1]
    rows = tokens // POOL
    kv_heads = kv_width // HEAD
    twice = lambda w: jnp.concatenate([w, w], axis=0)
    sems = 2 * (3 + 2 * (nz - 1) + 6) + 5 + ny + 4 * ny + 1
    vmem = pl.BlockSpec(memory_space=pltpu.VMEM)
    return pl.pallas_call(
        functools.partial(kernel, ny, nz),
        out_shape=jax.ShapeDtypeStruct((tokens, width), BF),
        in_specs=[vmem] * 8,
        out_specs=vmem,
        scratch_shapes=[
            pltpu.VMEM((2, nz, NX, rows, 2 * HEAD), BF),
            pltpu.VMEM((2, NX, nz, rows, 2 * HEAD), BF),
            pltpu.VMEM((tokens, kv_width), BF),
            pltpu.VMEM((tokens, kv_width), BF),
            pltpu.VMEM((tokens, kv_width), BF),
            pltpu.VMEM((tokens, kv_width), BF),
            pltpu.VMEM((QUERY_ROWS, width), BF),
            pltpu.VMEM((ny, rows, width), BF),
            pltpu.VMEM((ny, kv_heads, 4 * rows, 2 * HEAD), BF),
            pltpu.VMEM((kv_heads, ny, 4 * rows, 2 * HEAD), F32),
            pltpu.VMEM((kv_heads, ny, 4 * rows, HEAD), F32),
            pltpu.VMEM((2, ny, rows, width // 2), BF),
            pltpu.VMEM((2, ny, rows, width // 2), BF),
            pltpu.VMEM((2, ny, rows, HEAD), F32),
            pltpu.VMEM((2, ny, rows, HEAD), F32),
            pltpu.VMEM((tokens, width), F32),
            pltpu.VMEM((tokens, 3 * tokens), F32),
            pltpu.VMEM((tokens, HEAD), F32),
            pltpu.VMEM((tokens, HEAD), F32),
            pltpu.SemaphoreType.DMA((sems,)),
            pltpu.SemaphoreType.DMA((sems,)),
        ],
        compiler_params=pltpu.CompilerParams(collective_id=0, has_side_effects=True),
    )(queries, keys, values, twice(qw), twice(kw), twice(vw), twice(up), gain[None])


def solution(mesh):
    return jax.shard_map(
        functools.partial(per_device, mesh.shape["section"], mesh.shape["seq"]),
        mesh=mesh,
        in_specs=(
            P(("section", "seq"), "head"),
            P(("section", "seq"), "head"),
            P(("section", "seq"), "head"),
            P(None, "head"),
            P(None, "head"),
            P(None, "head"),
            P(None, "head"),
            P("head"),
        ),
        out_specs=P(("section", "seq"), "head"),
        check_vma=False,
    )
```

time: 381 us -> 118 us (0.31)
  the two profiles are of different devices: /device:TPU:31 before, /device:TPU:39 now
where the time goes in v1:
time: 118 us; the launch traced here: 117 us
  Pallas kernels  112 us (95%)
  other arithmetic  2.9 us (2%)
  local copies, waits for them, and re-layouts  2.31 us (2%)
    pallas_call x1, Pallas kernels, per_device(): pl.pallas_call(functools.partial(kernel, ny, nz), out_shape=jax.ShapeDtyp...  112 us
    concatenate x2, other arithmetic, per_device(): twice = lambda w: jnp.concatenate([w, w], axis=0)  2.9 us

profile of v1, /device:TPU:39, one launch (start us, length us, event | category | flops | bytes accessed | tf_op | source)
XLA Modules:
  0.0 117.4 jit_solution(3317181874837007888)
XLA Ops:
  0.0 0.0 copy-start
  0.0 1.4 %pad_maximum_fusion.2 = (f32[8,512]{1,0:T(8,128)}, f32[8,512]{1,0:T(8,128)}) fusion(f32[4,512]{1,0:T(4,128)} %param.12, f32[4,512]{1,0:T(4,128)} %param.13), kind=kLoop, calls=%fused_computation.2 | loop fusion | flops 8192 | bytes 49152 | tf_op jit(solution)/shard_map/concatenate | solution.py:452
  1.4 0.0 copy-done
  1.4 1.5 %pad_maximum_fusion = (f32[8,2048]{1,0:T(8,128)}, f32[8,2048]{1,0:T(8,128)}) fusion(f32[4,2048]{1,0:T(4,128)S(1)} %copy-done, f32[4,2048]{1,0:T(4,128)} %param.14), kind=kLoop, calls=%fused_computation | loop fusion | flops 32768 | bytes 196608 | tf_op jit(solution)/shard_map/concatenate | solution.py:452
  2.9 112.2 %shard_map.82 = bf16[256,2048]{1,0:T(8,128)(2,1)} custom-call(bf16[256,2048]{1,0:T(8,128)(2,1)} %q_ref.1, bf16[256,512]{1,0:T(8,128)(2,1)} %k_ref.1, bf16[256,512]{1,0:T(8,128)(2,1)} %v_ref.1, f32[8,2048]{1,0:T(8,128)} %get-tuple-element.5.qw_ref, f32[8,512]{1,0:T(8,128)} %get-tuple-element.7.kw_ref, f32[8,512]{1,0:T(8,128)} %get-tuple-element.8.vw_ref, ...), custom_call_target="tpu_custom_call" | custom-call | tf_op jit(solution)/shard_map/pallas_call | solution.py:455
  115.1 2.3 %copy.10 = bf16[256,2048]{1,0:T(8,128)(2,1)} copy(bf16[256,2048]{1,0:T(8,128)(2,1)} %shard_map.82) | data formatting | bytes 2097152
Async XLA Ops:
  0.0 1.4 %copy-start = (f32[4,2048]{1,0:T(4,128)S(1)}, f32[4,2048]{1,0:T(4,128)}, u32[]{:S(2)}) copy-start(f32[4,2048]{1,0:T(4,128)} %param.11) | copy-start | bytes 98308

commit v2 on v1

v2 whole, which is shorter than its diff:
```python
import functools

import jax
import jax.numpy as jnp
from jax import lax
from jax.experimental import pallas as pl
from jax.experimental.pallas import tpu as pltpu
from jax.sharding import PartitionSpec as P

MESH = pl.DeviceIdType.MESH
HEAD = 128
POOL = 4
WINDOW = 512
NX = 4
QUERY_ROWS = 16
SCALE = 1.4426950408889634 * HEAD ** -0.5
MASKED = -1e30
FLOOR = -1e29
BF = jnp.bfloat16
F32 = jnp.float32


def split_pair(value):
    high = value.astype(BF)
    low = (value - high.astype(F32)).astype(BF)
    return high, low


def dot(a, b):
    return lax.dot_general(a, b, (((1,), (0,)), ((), ())), preferred_element_type=F32)


def dot_t(a, b):
    return lax.dot_general(a, b, (((1,), (1,)), ((), ())), preferred_element_type=F32)


def iota(shape, dim):
    return lax.broadcasted_iota(jnp.int32, shape, dim)


def one_hot_groups(rows, columns, period, offset):
    r = iota((rows, columns), 0)
    c = lax.rem(iota((rows, columns), 1), period)
    first = c - offset - POOL * r
    return jnp.where((first >= 0) & (first < POOL), 1.0, 0.0).astype(BF)


def weighted_pair(rows, weights8):
    count, columns = rows.shape
    product = (rows.astype(F32).reshape(count // 8, 8, columns) * weights8[None]).reshape(count, columns)
    high, low = split_pair(product)
    return jnp.concatenate([high, low], axis=0)


def kernel(ny, nz, q_ref, k_ref, v_ref, qw_ref, kw_ref, vw_ref, up_ref, gain_ref, out_ref,
           ga, gb, hk1, hv1, hk2, hv2, hq, qall, qhl, acc, mst, osend, orecv, s0, s1,
           w0, w1, fine, bias, ssq, ssq_in, send_sem, recv_sem):
    tokens = q_ref.shape[0]
    rows = tokens // POOL
    y = lax.axis_index("section")
    s = lax.axis_index("seq")
    h = lax.axis_index("head")
    ns = NX * nz
    z = lax.div(s, NX)
    x = lax.rem(s, NX)
    position = y * ns + s
    plus_steps = 2
    minus_steps = nz - 1 - plus_steps

    def wrap(value, size):
        return lax.rem(value + 2 * size, size)

    def at(zz, xx):
        return (y, zz * NX + xx, h)

    def at_position(pp):
        return (lax.div(pp, ns), lax.rem(pp, ns), h)

    x_next, x_prev, x_far = wrap(x + 1, NX), wrap(x - 1, NX), wrap(x + 2, NX)
    right, left = at(z, x_next), at(z, x_prev)
    above, below = at(wrap(z + 1, nz), x), at(wrap(z - 1, nz), x)
    following = at_position(lax.rem(position + 1, ny * ns))
    preceding = at_position(lax.rem(position + ny * ns - 1, ny * ns))
    partner = (y, s, 1 - h)

    barrier = pltpu.get_barrier_semaphore()
    peers = [right, left, above, below, following, preceding, partner]
    peers += [(lax.rem(y + step, ny), s, h) for step in range(1, ny)]
    both = lambda w: jnp.concatenate([w, w], axis=0)
    for peer in peers:
        pl.semaphore_signal(barrier, inc=1, device_id=peer, device_id_type=MESH)

    per_wave = 3 + 2 * (nz - 1) + 6
    ax0, az0, bz0, bx0 = 0, 3, 3 + (nz - 1), 3 + 2 * (nz - 1)
    halo0 = 2 * per_wave
    q0 = halo0 + 5
    o0 = q0 + ny
    norm0 = o0 + 4 * ny

    def remote(src, dst, send_index, recv_index, device):
        return pltpu.make_async_remote_copy(
            src_ref=src, dst_ref=dst, send_sem=send_sem.at[send_index],
            recv_sem=recv_sem.at[recv_index], device_id=device, device_id_type=MESH)

    unconditional = []

    def send(ref, index, device, dst=None, key=None):
        copy = remote(ref, ref if dst is None else dst, index if key is None else key, index, device)
        copy.start()
        unconditional.append(copy)

    def arrived(ref, index):
        remote(ref, ref, index, index, left).wait_recv()

    pool_plain = one_hot_groups(rows, 2 * tokens, tokens, 0)
    for wave in range(2):
        for kind in range(2):
            kv = 2 * wave + kind
            columns = slice(kv * HEAD, (kv + 1) * HEAD)
            pooled_k = dot(pool_plain, weighted_pair(k_ref[:, columns], both(kw_ref[:, columns]))).astype(BF)
            pooled_v = dot(pool_plain, weighted_pair(v_ref[:, columns], both(vw_ref[:, columns]))).astype(BF)
            block = jnp.concatenate([pooled_k, pooled_v], axis=1)
            if kind == 0:
                ga[wave, z, x] = block
            else:
                gb[wave, x, z] = block
    pl.semaphore_wait(barrier, len(peers))

    def ax_start(w):
        base = w * per_wave + ax0
        send(ga.at[w, z, x], base + 1, left)
        send(ga.at[w, z, x], base + 0, right)

    def ax_rest(w):
        base = w * per_wave + ax0
        arrived(ga.at[w, z, x_next], base + 1)
        send(ga.at[w, z, x_next], base + 2, left)
        arrived(ga.at[w, z, x_prev], base + 0)
        arrived(ga.at[w, z, x_far], base + 2)

    def z_plus(ref_at, base, d):
        if d > 0:
            arrived(ref_at(wrap(z - d, nz)), base + d - 1)
        if d < plus_steps:
            send(ref_at(wrap(z - d, nz)), base + d, above)

    def z_minus(ref_at, base, d):
        base = base + plus_steps
        if d > 0:
            arrived(ref_at(wrap(z + d, nz)), base + d - 1)
        if d < minus_steps:
            send(ref_at(wrap(z + d, nz)), base + d, below)

    def az(w, d):
        ref_at = lambda zz: ga.at[w, zz]
        if d <= minus_steps:
            z_minus(ref_at, w * per_wave + az0, d)
        if d <= plus_steps:
            z_plus(ref_at, w * per_wave + az0, d)

    def bz(w, d):
        ref_at = lambda zz: gb.at[w, x, zz]
        if d <= minus_steps:
            z_minus(ref_at, w * per_wave + bz0, d)
        if d <= plus_steps:
            z_plus(ref_at, w * per_wave + bz0, d)

    half_rows = nz // 2

    def half_of(w, xx, half):
        return gb.at[w, xx, pl.ds(half * half_rows, half_rows)]

    def bx_start(w, half):
        base = w * per_wave + bx0 + 3 * half
        send(half_of(w, x, half), base + 1, left)
        send(half_of(w, x, half), base + 0, right)

    def bx_relay(w, half):
        base = w * per_wave + bx0 + 3 * half
        arrived(half_of(w, x_next, half), base + 1)
        send(half_of(w, x_next, half), base + 2, left)

    def bx_rest(w, half):
        base = w * per_wave + bx0 + 3 * half
        arrived(half_of(w, x_prev, half), base + 0)
        arrived(half_of(w, x_far, half), base + 2)

    send(q_ref.at[pl.ds(tokens - QUERY_ROWS, QUERY_ROWS)], halo0 + 4, following, hq)
    for w in range(2):
        ax_start(w)
        bz(w, 0)
    send(k_ref, halo0 + 0, following, hk1)
    send(v_ref, halo0 + 1, following, hv1)

    r = iota((tokens, tokens), 0)
    c = iota((tokens, tokens), 1)
    bias[:, 0:tokens] = jnp.where((c > r) & (position >= 2), 0.0, MASKED)
    bias[:, tokens:2 * tokens] = jnp.where((c >= 0) & (position >= 1), 0.0, MASKED)
    bias[:, 2 * tokens:3 * tokens] = jnp.where(c <= r, 0.0, MASKED)

    arrived(hq, halo0 + 4)
    pool_shifted = one_hot_groups(rows, 2 * (tokens + QUERY_ROWS), tokens + QUERY_ROWS, QUERY_ROWS - POOL)
    heads = q_ref.shape[1] // HEAD

    def pool_head(n, carry):
        columns = pl.ds(pl.multiple_of(n * HEAD, HEAD), HEAD)
        joined = jnp.concatenate([hq[:, columns], q_ref[:, columns]], axis=0)
        pooled = dot(pool_shifted, weighted_pair(joined, both(qw_ref[:, columns]))).astype(BF)
        qall[y, :, columns] = pooled
        return carry

    lax.fori_loop(0, heads, pool_head, 0)

    def prepare(j):
        def one(n, carry):
            columns = pl.ds(pl.multiple_of(n * HEAD, HEAD), HEAD)
            high, low = split_pair(qall[y + j, :, columns].astype(F32) * SCALE)
            group = pl.ds(pl.multiple_of(lax.rem(n, 4) * rows, rows), rows)
            qhl[j, lax.div(n, 4), group, :] = jnp.concatenate([high, low], axis=1)
            return carry

        lax.fori_loop(0, heads, one, 0)

    def query_copy(t, target, index):
        return remote(qall.at[t], qall.at[t], q0 + index, q0 + t, (target, s, h))

    @pl.when(y > 0)
    def _():
        query_copy(y, y - 1, 0).start()

    @pl.when(y == ny - 1)
    def _():
        query_copy(y, 0, 1).start()

    bz(0, 1)
    bz(1, 1)
    ax_rest(0)
    az(0, 0)
    bz(0, 2)
    bz(1, 2)
    ax_rest(1)
    az(1, 0)
    prepare(0)
    bz(0, 3)
    bz(1, 3)
    az(0, 1)

    @pl.when(y == 1)
    def _():
        arrived(qall.at[2], q0 + 2)
        query_copy(2, 0, 2).start()

    @pl.when(y == 0)
    def _():
        arrived(qall.at[ny - 1], q0 + ny - 1)
        query_copy(ny - 1, 1, 2).start()

    bz(0, 4)
    bz(1, 4)
    az(1, 1)
    bz(0, 5)
    for half in range(2):
        bx_start(0, half)
    bz(1, 5)
    az(0, 2)

    def coarse(kv, keys, values, key_position, first):
        keys = jnp.concatenate([keys, keys], axis=1)
        values = jnp.concatenate([values, jnp.ones_like(values)], axis=1)
        limit = rows * s + lax.rem(iota((4 * rows, 1), 0), rows)
        buffers = (s0, s1)
        s0[...] = dot_t(qhl[0, kv], keys)
        for j in range(ny):
            if j + 1 < ny:
                buffers[(j + 1) % 2][...] = dot_t(qhl[j + 1, kv], keys)
            scores = buffers[j % 2][...]
            if j == 0:
                scores = jnp.where(key_position < limit, scores, MASKED)
            newest = jnp.max(scores, axis=1, keepdims=True)
            if first:
                top = jnp.maximum(newest, FLOOR)
                newest = jnp.broadcast_to(top, (4 * rows, HEAD))
            else:
                before = mst[kv, j]
                newest = jnp.maximum(before, newest)
                top = newest[:, :1]
            mst[kv, j] = newest
            blended = dot(jnp.exp2(scores - top).astype(BF), values)
            if first:
                acc[kv, j] = blended
            else:
                shrink = jnp.exp2(before - newest)
                acc[kv, j] = acc[kv, j] * jnp.concatenate([shrink, shrink], axis=1) + blended

    def coarse_a(w, steps, first=False):
        count = NX * rows
        places = [wrap(z + d, nz) for d in steps]
        block = jnp.concatenate([ga[w, zz].reshape(count, 2 * HEAD) for zz in places], axis=0)
        position = jnp.concatenate([zz * count + iota((1, count), 1) for zz in places], axis=1)
        coarse(2 * w, block[:, :HEAD], block[:, HEAD:], position, first)

    def coarse_b(w, half, first=False):
        block = gb[w, :, half * half_rows:(half + 1) * half_rows].reshape(NX * half_rows * rows, 2 * HEAD)
        index = iota((1, NX * half_rows * rows), 1)
        xx = lax.div(index, half_rows * rows)
        zz = lax.rem(lax.div(index, rows), half_rows) + half * half_rows
        position = (zz * NX + xx) * rows + lax.rem(index, rows)
        coarse(2 * w + 1, block[:, :HEAD], block[:, HEAD:], position, first)

    def finish(kv):
        lane = iota((rows, HEAD), 1)
        for j in range(1, ny):
            @pl.when(y + j < ny)
            def _():
                stats = jnp.zeros((rows, HEAD), F32)
                for g in range(4):
                    part = slice(g * rows, (g + 1) * rows)
                    total = acc[kv, j, part, HEAD:]
                    osend[kv, j, :, g * HEAD:(g + 1) * HEAD] = (acc[kv, j, part, :HEAD] / total).astype(BF)
                    level = mst[kv, j, part] + jnp.log2(total)
                    high, low = split_pair(level)
                    rest = level - high.astype(F32) - low.astype(F32)
                    stats = jnp.where(lane == g, high.astype(F32), stats)
                    stats = jnp.where(lane == 4 + g, low.astype(F32), stats)
                    stats = jnp.where(lane == 8 + g, rest, stats)
                osend[kv, j, :, 4 * HEAD:] = stats.astype(BF)

    def partial_copy(kv, j):
        base = o0 + kv * ny
        return remote(osend.at[kv, j], orecv.at[kv, y], base + j, base + y, (y + j, s, h))

    def send_partials(kv):
        for j in range(1, ny):
            @pl.when(y + j < ny)
            def _():
                partial_copy(kv, j).start()

    def window(kv):
        part = slice(kv * HEAD, (kv + 1) * HEAD)
        keys = jnp.concatenate([hk2[:, part], hk1[:, part], k_ref[:, part]], axis=0)
        values = jnp.concatenate([hv2[:, part], hv1[:, part], v_ref[:, part]], axis=0)
        keys = jnp.concatenate([keys, keys], axis=1)
        values = jnp.concatenate([values, jnp.ones_like(values)], axis=1)
        buffers = (w0, w1)

        def scores_of(g):
            high, low = split_pair(q_ref[:, (4 * kv + g) * HEAD:(4 * kv + g + 1) * HEAD].astype(F32) * SCALE)
            buffers[g % 2][...] = dot_t(jnp.concatenate([high, low], axis=1), keys)

        scores_of(0)
        for g in range(4):
            if g < 3:
                scores_of(g + 1)
            scores = buffers[g % 2][...] + bias[...]
            weights = jnp.exp2(scores - jnp.max(scores, axis=1, keepdims=True)).astype(BF)
            blended = dot(weights, values)
            fine[:, (4 * kv + g) * HEAD:(4 * kv + g + 1) * HEAD] = blended[:, :HEAD] / blended[:, HEAD:]

    arrived(hk1, halo0 + 0)
    send(hk1, halo0 + 2, following, hk2)
    arrived(hv1, halo0 + 1)
    send(hv1, halo0 + 3, following, hv2)
    for half in range(2):
        bx_start(1, half)
    az(1, 2)

    @pl.when(y == 0)
    def _():
        arrived(qall.at[1], q0 + 1)
        arrived(qall.at[2], q0 + 2)

    @pl.when((y == 1) | (y == 2))
    def _():
        arrived(qall.at[ny - 1], q0 + ny - 1)

    for j in range(1, ny):
        @pl.when(y + j < ny)
        def _():
            prepare(j)

        @pl.when(y + j >= ny)
        def _():
            qhl[j] = jnp.zeros(qhl.shape[1:], BF)

    for half in range(2):
        bx_relay(0, half)
    az(0, 3)
    coarse_a(0, (0, -1, 1, 2), True)
    az(1, 3)
    bx_rest(0, 0)
    coarse_b(0, 0, True)
    az(0, 4)
    bx_rest(0, 1)
    for half in range(2):
        bx_relay(1, half)
    coarse_b(0, 1)
    az(1, 4)
    finish(1)
    send_partials(1)
    coarse_a(1, (0, -1, 1, 2), True)
    az(0, 5)
    coarse_a(0, (-2, 3, 4, 5))
    finish(0)
    send_partials(0)
    az(1, 5)
    coarse_a(1, (-2, 3, 4, 5))
    finish(2)
    send_partials(2)
    bx_rest(1, 0)
    coarse_b(1, 0, True)
    bx_rest(1, 1)
    coarse_b(1, 1)
    finish(3)
    send_partials(3)
    arrived(hk2, halo0 + 2)
    arrived(hv2, halo0 + 3)
    for kv in range(4):
        window(kv)

    for kv in range(4):
        for src in range(ny - 1):
            @pl.when(src < y)
            def _():
                arrived(orecv.at[kv, src], o0 + kv * ny + src)

    expand = jnp.where(
        lax.rem(iota((tokens, 2 * rows), 1), rows) == lax.div(iota((tokens, 2 * rows), 0), POOL), 1.0, 0.0).astype(BF)
    squares = jnp.zeros((tokens, HEAD), F32)
    for w in range(2):
        for kind in range(2):
            kv = 2 * w + kind
            for g in range(4):
                part = slice(g * rows, (g + 1) * rows)
                state = (mst[kv, 0, part], acc[kv, 0, part, :HEAD], acc[kv, 0, part, HEAD:])

                def join(src, state):
                    top, number, total = state
                    stats = orecv[kv, src, :, 4 * HEAD:].astype(F32)
                    other = stats[:, g:g + 1] + stats[:, 4 + g:5 + g] + stats[:, 8 + g:9 + g]
                    other = jnp.broadcast_to(other, (rows, HEAD))
                    newest = jnp.maximum(top, other)
                    mine, theirs = jnp.exp2(top - newest), jnp.exp2(other - newest)
                    blended = orecv[kv, src, :, g * HEAD:(g + 1) * HEAD].astype(F32)
                    return newest, number * mine + blended * theirs, total * mine + theirs

                top, number, total = lax.fori_loop(0, y, join, state)
                coarse_out = jnp.where(total > 0.0, number / jnp.where(total > 0.0, total, 1.0), 0.0)
                high, low = split_pair(coarse_out)
                spread = dot(expand, jnp.concatenate([high, low], axis=0))
                columns = slice((kv * 4 + g) * HEAD, (kv * 4 + g + 1) * HEAD)
                lifted = (spread.reshape(tokens // 8, 8, HEAD) * both(up_ref[:, columns])[None]).reshape(tokens, HEAD)
                combined = fine[:, columns] + lifted
                fine[:, columns] = combined
                squares = squares + combined * combined
    ssq[...] = squares
    send(ssq, norm0, partner, ssq_in)
    arrived(ssq_in, norm0)
    mean = jnp.sum(squares + ssq_in[...], axis=1, keepdims=True) / (2.0 * q_ref.shape[1])
    factor = jnp.broadcast_to(lax.rsqrt(mean + 1e-05), (tokens, HEAD))
    for n in range(heads):
        columns = slice(n * HEAD, (n + 1) * HEAD)
        out_ref[:, columns] = (fine[:, columns] * factor * gain_ref[:, columns]).astype(BF)

    for copy in unconditional:
        copy.wait_send()
    @pl.when(y > 0)
    def _():
        query_copy(y, y - 1, 0).wait_send()

    @pl.when(y == ny - 1)
    def _():
        query_copy(y, 0, 1).wait_send()

    @pl.when(y == 1)
    def _():
        query_copy(2, 0, 2).wait_send()

    @pl.when(y == 0)
    def _():
        query_copy(ny - 1, 1, 2).wait_send()

    for kv in range(4):
        for j in range(1, ny):
            @pl.when(y + j < ny)
            def _():
                partial_copy(kv, j).wait_send()


def per_device(ny, ns, queries, keys, values, qw, kw, vw, up, gain):
    nz = ns // NX
    tokens, width = queries.shape
    kv_width = keys.shape[1]
    rows = tokens // POOL
    kv_heads = kv_width // HEAD
    sems = 2 * (3 + 2 * (nz - 1) + 6) + 5 + ny + 4 * ny + 1
    vmem = pl.BlockSpec(memory_space=pltpu.VMEM)
    return pl.pallas_call(
        functools.partial(kernel, ny, nz),
        out_shape=jax.ShapeDtypeStruct((tokens, width), BF),
        in_specs=[vmem] * 8,
        out_specs=vmem,
        scratch_shapes=[
            pltpu.VMEM((2, nz, NX, rows, 2 * HEAD), BF),
            pltpu.VMEM((2, NX, nz, rows, 2 * HEAD), BF),
            pltpu.VMEM((tokens, kv_width), BF),
            pltpu.VMEM((tokens, kv_width), BF),
            pltpu.VMEM((tokens, kv_width), BF),
            pltpu.VMEM((tokens, kv_width), BF),
            pltpu.VMEM((QUERY_ROWS, width), BF),
            pltpu.VMEM((ny, rows, width), BF),
            pltpu.VMEM((ny, kv_heads, 4 * rows, 2 * HEAD), BF),
            pltpu.VMEM((kv_heads, ny, 4 * rows, 2 * HEAD), F32),
            pltpu.VMEM((kv_heads, ny, 4 * rows, HEAD), F32),
            pltpu.VMEM((kv_heads, ny, rows, 5 * HEAD), BF),
            pltpu.VMEM((kv_heads, ny, rows, 5 * HEAD), BF),
            pltpu.VMEM((4 * rows, NX * nz * rows // 2), F32),
            pltpu.VMEM((4 * rows, NX * nz * rows // 2), F32),
            pltpu.VMEM((tokens, 3 * tokens), F32),
            pltpu.VMEM((tokens, 3 * tokens), F32),
            pltpu.VMEM((tokens, width), F32),
            pltpu.VMEM((tokens, 3 * tokens), F32),
            pltpu.VMEM((tokens, HEAD), F32),
            pltpu.VMEM((tokens, HEAD), F32),
            pltpu.SemaphoreType.DMA((sems,)),
            pltpu.SemaphoreType.DMA((sems,)),
        ],
        compiler_params=pltpu.CompilerParams(collective_id=0, has_side_effects=True),
    )(queries, keys, values, qw, kw, vw, up, gain[None])


def solution(mesh):
    return jax.shard_map(
        functools.partial(per_device, mesh.shape["section"], mesh.shape["seq"]),
        mesh=mesh,
        in_specs=(
            P(("section", "seq"), "head"),
            P(("section", "seq"), "head"),
            P(("section", "seq"), "head"),
            P(None, "head"),
            P(None, "head"),
            P(None, "head"),
            P(None, "head"),
            P("head"),
        ),
        out_specs=P(("section", "seq"), "head"),
        check_vma=False,
    )
```

time: 118 us -> 88.7 us (0.75)
  the two profiles are of different devices: /device:TPU:39 before, /device:TPU:31 now
where the time goes in v2:
time: 88.7 us; the launch traced here: 88.5 us
  Pallas kernels  86.2 us (97%)
  local copies, waits for them, and re-layouts  2.3 us (3%)
    pallas_call x1, Pallas kernels, per_device(): pl.pallas_call(functools.partial(kernel, ny, nz), out_shape=jax.ShapeDtyp...  86.2 us
    unnamed x1, local copies, waits for them, and re-layouts  2.3 us

profile of v2, /device:TPU:31, one launch (start us, length us, event | category | flops | bytes accessed | tf_op | source)
XLA Modules:
  0.0 88.5 jit_solution(5208303590690977740)
XLA Ops:
  0.0 86.2 %shard_map.82 = bf16[256,2048]{1,0:T(8,128)(2,1)} custom-call(bf16[256,2048]{1,0:T(8,128)(2,1)} %q_ref.1, bf16[256,512]{1,0:T(8,128)(2,1)} %k_ref.1, bf16[256,512]{1,0:T(8,128)(2,1)} %v_ref.1, f32[4,2048]{1,0:T(4,128)} %qw_ref.1, f32[4,512]{1,0:T(4,128)} %kw_ref.1, f32[4,512]{1,0:T(4,128)} %vw_ref.1, f32[4,2048]{1,0:T(4,128)} %up_ref.1, f32[1,2048]{1,0:T(1,128)} %bitcast.1), custom_call_target="tpu_custom_call" | custom-call | tf_op jit(solution)/shard_map/pallas_call | solution.py:497
  86.2 2.3 %copy.10 = bf16[256,2048]{1,0:T(8,128)(2,1)} copy(bf16[256,2048]{1,0:T(8,128)(2,1)} %shard_map.82) | data formatting | bytes 2097152

commit v3 on v2

--- a/solution.py
+++ b/solution.py
@@ -18,6 +18,28 @@
 FLOOR = -1e29
 BF = jnp.bfloat16
 F32 = jnp.float32
+ORDER = (
+    "hq as0 B0 B1",
+    "hsk as1 ar0 B2",
+    "PQ B3 a010 hsv",
+    "qs ar1 B4 a000",
+    "a110 BI B5 a011",
+    "bs00 bs01 bs11 qr",
+    "a100 a001 br00 bs10",
+    "a111 a012 a101 a002",
+    "a013 a003 br01 hrv",
+    "qw PR hrk bw00",
+    "a102 a112 a014 UA00",
+    "br11 UB00 a004 a103",
+    "UA10 a113 bw01 br10",
+    "UB01 bw11 F1 a005",
+    "a015 UA01 hwv a114",
+    "a104 F0 bw10 UB10",
+    "UB11 hwk a115 a105",
+    "F3 UA11 F2 W2",
+    "W1 W0 W3 J1",
+    "J0 J2 J3",
+)
 
 
 def split_pair(value):
@@ -38,11 +60,10 @@
     return lax.broadcasted_iota(jnp.int32, shape, dim)
 
 
-def one_hot_groups(rows, columns, period, offset):
-    r = iota((rows, columns), 0)
-    c = lax.rem(iota((rows, columns), 1), period)
-    first = c - offset - POOL * r
-    return jnp.where((first >= 0) & (first < POOL), 1.0, 0.0).astype(BF)
+def one_hot_groups(rows, columns, offset):
+    first = iota((rows, columns), 1) - offset - POOL * iota((rows, columns), 0)
+    base = jnp.where((first >= 0) & (first < POOL), 1.0, 0.0).astype(BF)
+    return jnp.concatenate([base, base], axis=1)
 
 
 def weighted_pair(rows, weights8):
@@ -52,7 +73,7 @@
     return jnp.concatenate([high, low], axis=0)
 
 
-def kernel(ny, nz, q_ref, k_ref, v_ref, qw_ref, kw_ref, vw_ref, up_ref, gain_ref, out_ref,
+def kernel(ny, nz, order, q_ref, k_ref, v_ref, qw_ref, kw_ref, vw_ref, up_ref, gain_ref, out_ref,
            ga, gb, hk1, hv1, hk2, hv2, hq, qall, qhl, acc, mst, osend, orecv, s0, s1,
            w0, w1, fine, bias, ssq, ssq_in, send_sem, recv_sem):
     tokens = q_ref.shape[0]
@@ -90,9 +111,11 @@
     for peer in peers:
         pl.semaphore_signal(barrier, inc=1, device_id=peer, device_id_type=MESH)
 
-    per_wave = 3 + 2 * (nz - 1) + 6
-    ax0, az0, bz0, bx0 = 0, 3, 3 + (nz - 1), 3 + 2 * (nz - 1)
-    halo0 = 2 * per_wave
+    ax0 = 0
+    az0 = ax0 + 2 * 3
+    bz0 = az0 + 4 * (nz - 1)
+    bx0 = bz0 + nz - 1
+    halo0 = bx0 + 4 * 3
     q0 = halo0 + 5
     o0 = q0 + ny
     norm0 = o0 + 4 * ny
@@ -112,14 +135,13 @@
     def arrived(ref, index):
         remote(ref, ref, index, index, left).wait_recv()
 
-    pool_plain = one_hot_groups(rows, 2 * tokens, tokens, 0)
+    pool_plain = one_hot_groups(rows, tokens, 0)
+    pooled_k = dot(pool_plain, weighted_pair(k_ref[...], both(kw_ref[...]))).astype(BF)
+    pooled_v = dot(pool_plain, weighted_pair(v_ref[...], both(vw_ref[...]))).astype(BF)
     for wave in range(2):
         for kind in range(2):
-            kv = 2 * wave + kind
-            columns = slice(kv * HEAD, (kv + 1) * HEAD)
-            pooled_k = dot(pool_plain, weighted_pair(k_ref[:, columns], both(kw_ref[:, columns]))).astype(BF)
-            pooled_v = dot(pool_plain, weighted_pair(v_ref[:, columns], both(vw_ref[:, columns]))).astype(BF)
-            block = jnp.concatenate([pooled_k, pooled_v], axis=1)
+            columns = slice((2 * wave + kind) * HEAD, (2 * wave + kind + 1) * HEAD)
+            block = jnp.concatenate([pooled_k[:, columns], pooled_v[:, columns]], axis=1)
             if kind == 0:
                 ga[wave, z, x] = block
             else:
@@ -127,43 +149,35 @@
     pl.semaphore_wait(barrier, len(peers))
 
     def ax_start(w):
-        base = w * per_wave + ax0
+        base = ax0 + 3 * w
         send(ga.at[w, z, x], base + 1, left)
         send(ga.at[w, z, x], base + 0, right)
 
     def ax_rest(w):
-        base = w * per_wave + ax0
+        base = ax0 + 3 * w
         arrived(ga.at[w, z, x_next], base + 1)
         send(ga.at[w, z, x_next], base + 2, left)
         arrived(ga.at[w, z, x_prev], base + 0)
         arrived(ga.at[w, z, x_far], base + 2)
 
-    def z_plus(ref_at, base, d):
-        if d > 0:
-            arrived(ref_at(wrap(z - d, nz)), base + d - 1)
-        if d < plus_steps:
-            send(ref_at(wrap(z - d, nz)), base + d, above)
-
-    def z_minus(ref_at, base, d):
-        base = base + plus_steps
-        if d > 0:
-            arrived(ref_at(wrap(z + d, nz)), base + d - 1)
-        if d < minus_steps:
-            send(ref_at(wrap(z + d, nz)), base + d, below)
-
-    def az(w, d):
-        ref_at = lambda zz: ga.at[w, zz]
+    def along_z(ref_at, base, d):
+        low = base + plus_steps
         if d <= minus_steps:
-            z_minus(ref_at, w * per_wave + az0, d)
+            if d > 0:
+                arrived(ref_at(wrap(z + d, nz)), low + d - 1)
+            if d < minus_steps:
+                send(ref_at(wrap(z + d, nz)), low + d, below)
         if d <= plus_steps:
-            z_plus(ref_at, w * per_wave + az0, d)
-
-    def bz(w, d):
-        ref_at = lambda zz: gb.at[w, x, zz]
-        if d <= minus_steps:
-            z_minus(ref_at, w * per_wave + bz0, d)
-        if d <= plus_steps:
-            z_plus(ref_at, w * per_wave + bz0, d)
+            if d > 0:
+                arrived(ref_at(wrap(z - d, nz)), base + d - 1)
+            if d < plus_steps:
+                send(ref_at(wrap(z - d, nz)), base + d, above)
+
+    def az(w, part, d):
+        along_z(lambda zz: ga.at[w, zz, pl.ds(part * (NX // 2), NX // 2)], az0 + (2 * w + part) * (nz - 1), d)
+
+    def bz(d):
+        along_z(lambda zz: gb.at[:, x, zz], bz0, d)
 
     half_rows = nz // 2
 
@@ -171,98 +185,115 @@
         return gb.at[w, xx, pl.ds(half * half_rows, half_rows)]
 
     def bx_start(w, half):
-        base = w * per_wave + bx0 + 3 * half
+        base = bx0 + 3 * (2 * w + half)
         send(half_of(w, x, half), base + 1, left)
         send(half_of(w, x, half), base + 0, right)
 
     def bx_relay(w, half):
-        base = w * per_wave + bx0 + 3 * half
+        base = bx0 + 3 * (2 * w + half)
         arrived(half_of(w, x_next, half), base + 1)
         send(half_of(w, x_next, half), base + 2, left)
 
     def bx_rest(w, half):
-        base = w * per_wave + bx0 + 3 * half
+        base = bx0 + 3 * (2 * w + half)
         arrived(half_of(w, x_prev, half), base + 0)
         arrived(half_of(w, x_far, half), base + 2)
 
-    send(q_ref.at[pl.ds(tokens - QUERY_ROWS, QUERY_ROWS)], halo0 + 4, following, hq)
-    for w in range(2):
-        ax_start(w)
-        bz(w, 0)
-    send(k_ref, halo0 + 0, following, hk1)
-    send(v_ref, halo0 + 1, following, hv1)
-
-    r = iota((tokens, tokens), 0)
-    c = iota((tokens, tokens), 1)
-    bias[:, 0:tokens] = jnp.where((c > r) & (position >= 2), 0.0, MASKED)
-    bias[:, tokens:2 * tokens] = jnp.where((c >= 0) & (position >= 1), 0.0, MASKED)
-    bias[:, 2 * tokens:3 * tokens] = jnp.where(c <= r, 0.0, MASKED)
-
-    arrived(hq, halo0 + 4)
-    pool_shifted = one_hot_groups(rows, 2 * (tokens + QUERY_ROWS), tokens + QUERY_ROWS, QUERY_ROWS - POOL)
+    own, once, twice = (k_ref, v_ref), (hk1, hv1), (hk2, hv2)
+
+    def halo_start(which):
+        send(own[which], halo0 + which, following, once[which])
+
+    def halo_relay(which):
+        arrived(once[which], halo0 + which)
+        send(once[which], halo0 + 2 + which, following, twice[which])
+
+    def halo_rest(which):
+        arrived(twice[which], halo0 + 2 + which)
+
+    def halo_queries():
+        send(q_ref.at[pl.ds(tokens - QUERY_ROWS, QUERY_ROWS)], halo0 + 4, following, hq)
+
+    def window_masks():
+        r = iota((tokens, tokens), 0)
+        c = iota((tokens, tokens), 1)
+        bias[:, 0:tokens] = jnp.where((c > r) & (position >= 2), 0.0, MASKED)
+        bias[:, tokens:2 * tokens] = jnp.where((c >= 0) & (position >= 1), 0.0, MASKED)
+        bias[:, 2 * tokens:3 * tokens] = jnp.where(c <= r, 0.0, MASKED)
+
     heads = q_ref.shape[1] // HEAD
 
-    def pool_head(n, carry):
-        columns = pl.ds(pl.multiple_of(n * HEAD, HEAD), HEAD)
-        joined = jnp.concatenate([hq[:, columns], q_ref[:, columns]], axis=0)
-        pooled = dot(pool_shifted, weighted_pair(joined, both(qw_ref[:, columns]))).astype(BF)
-        qall[y, :, columns] = pooled
-        return carry
-
-    lax.fori_loop(0, heads, pool_head, 0)
+    def put_scaled(j, n, pooled):
+        high, low = split_pair(pooled.astype(F32) * SCALE)
+        group = pl.ds(pl.multiple_of(lax.rem(n, 4) * rows, rows), rows)
+        qhl[j, lax.div(n, 4), group, :] = jnp.concatenate([high, low], axis=1)
+
+    def pool_queries():
+        arrived(hq, halo0 + 4)
+        pool_shifted = one_hot_groups(rows, tokens + QUERY_ROWS, QUERY_ROWS - POOL)
+
+        def two_heads(i, carry):
+            columns = pl.ds(pl.multiple_of(i * 2 * HEAD, 2 * HEAD), 2 * HEAD)
+            joined = jnp.concatenate([hq[:, columns], q_ref[:, columns]], axis=0)
+            pooled = dot(pool_shifted, weighted_pair(joined, both(qw_ref[:, columns]))).astype(BF)
+            qall[y, :, columns] = pooled
+            put_scaled(0, 2 * i, pooled[:, :HEAD])
+            put_scaled(0, 2 * i + 1, pooled[:, HEAD:])
+            return carry
+
+        lax.fori_loop(0, heads // 2, two_heads, 0)
 
     def prepare(j):
-        def one(n, carry):
-            columns = pl.ds(pl.multiple_of(n * HEAD, HEAD), HEAD)
-            high, low = split_pair(qall[y + j, :, columns].astype(F32) * SCALE)
-            group = pl.ds(pl.multiple_of(lax.rem(n, 4) * rows, rows), rows)
-            qhl[j, lax.div(n, 4), group, :] = jnp.concatenate([high, low], axis=1)
+        def two_heads(i, carry):
+            for k in range(2):
+                n = 2 * i + k
+                put_scaled(j, n, qall[y + j, :, pl.ds(pl.multiple_of(n * HEAD, HEAD), HEAD)])
             return carry
 
-        lax.fori_loop(0, heads, one, 0)
+        lax.fori_loop(0, heads // 2, two_heads, 0)
 
     def query_copy(t, target, index):
         return remote(qall.at[t], qall.at[t], q0 + index, q0 + t, (target, s, h))
 
-    @pl.when(y > 0)
-    def _():
-        query_copy(y, y - 1, 0).start()
-
-    @pl.when(y == ny - 1)
-    def _():
-        query_copy(y, 0, 1).start()
-
-    bz(0, 1)
-    bz(1, 1)
-    ax_rest(0)
-    az(0, 0)
-    bz(0, 2)
-    bz(1, 2)
-    ax_rest(1)
-    az(1, 0)
-    prepare(0)
-    bz(0, 3)
-    bz(1, 3)
-    az(0, 1)
-
-    @pl.when(y == 1)
-    def _():
-        arrived(qall.at[2], q0 + 2)
-        query_copy(2, 0, 2).start()
-
-    @pl.when(y == 0)
-    def _():
-        arrived(qall.at[ny - 1], q0 + ny - 1)
-        query_copy(ny - 1, 1, 2).start()
-
-    bz(0, 4)
-    bz(1, 4)
-    az(1, 1)
-    bz(0, 5)
-    for half in range(2):
-        bx_start(0, half)
-    bz(1, 5)
-    az(0, 2)
+    def query_start():
+        @pl.when(y > 0)
+        def _():
+            query_copy(y, y - 1, 0).start()
+
+        @pl.when(y == ny - 1)
+        def _():
+            query_copy(y, 0, 1).start()
+
+    def query_relay():
+        @pl.when(y == 1)
+        def _():
+            arrived(qall.at[2], q0 + 2)
+            query_copy(2, 0, 2).start()
+
+        @pl.when(y == 0)
+        def _():
+            arrived(qall.at[ny - 1], q0 + ny - 1)
+            query_copy(ny - 1, 1, 2).start()
+
+    def query_rest():
+        @pl.when(y == 0)
+        def _():
+            arrived(qall.at[1], q0 + 1)
+            arrived(qall.at[2], q0 + 2)
+
+        @pl.when((y == 1) | (y == 2))
+        def _():
+            arrived(qall.at[ny - 1], q0 + ny - 1)
+
+    def prepare_rest():
+        for j in range(1, ny):
+            @pl.when(y + j < ny)
+            def _():
+                prepare(j)
+
+            @pl.when(y + j >= ny)
+            def _():
+                qhl[j] = jnp.zeros(qhl.shape[1:], BF)
 
     def coarse(kv, keys, values, key_position, first):
         keys = jnp.concatenate([keys, keys], axis=1)
@@ -356,106 +387,84 @@
             blended = dot(weights, values)
             fine[:, (4 * kv + g) * HEAD:(4 * kv + g + 1) * HEAD] = blended[:, :HEAD] / blended[:, HEAD:]
 
-    arrived(hk1, halo0 + 0)
-    send(hk1, halo0 + 2, following, hk2)
-    arrived(hv1, halo0 + 1)
-    send(hv1, halo0 + 3, following, hv2)
-    for half in range(2):
-        bx_start(1, half)
-    az(1, 2)
-
-    @pl.when(y == 0)
-    def _():
-        arrived(qall.at[1], q0 + 1)
-        arrived(qall.at[2], q0 + 2)
-
-    @pl.when((y == 1) | (y == 2))
-    def _():
-        arrived(qall.at[ny - 1], q0 + ny - 1)
-
-    for j in range(1, ny):
-        @pl.when(y + j < ny)
-        def _():
-            prepare(j)
-
-        @pl.when(y + j >= ny)
-        def _():
-            qhl[j] = jnp.zeros(qhl.shape[1:], BF)
-
-    for half in range(2):
-        bx_relay(0, half)
-    az(0, 3)
-    coarse_a(0, (0, -1, 1, 2), True)
-    az(1, 3)
-    bx_rest(0, 0)
-    coarse_b(0, 0, True)
-    az(0, 4)
-    bx_rest(0, 1)
-    for half in range(2):
-        bx_relay(1, half)
-    coarse_b(0, 1)
-    az(1, 4)
-    finish(1)
-    send_partials(1)
-    coarse_a(1, (0, -1, 1, 2), True)
-    az(0, 5)
-    coarse_a(0, (-2, 3, 4, 5))
-    finish(0)
-    send_partials(0)
-    az(1, 5)
-    coarse_a(1, (-2, 3, 4, 5))
-    finish(2)
-    send_partials(2)
-    bx_rest(1, 0)
-    coarse_b(1, 0, True)
-    bx_rest(1, 1)
-    coarse_b(1, 1)
-    finish(3)
-    send_partials(3)
-    arrived(hk2, halo0 + 2)
-    arrived(hv2, halo0 + 3)
-    for kv in range(4):
-        window(kv)
-
-    for kv in range(4):
+    expand = jnp.where(
+        lax.rem(iota((tokens, 2 * rows), 1), rows) == lax.div(iota((tokens, 2 * rows), 0), POOL), 1.0, 0.0).astype(BF)
+
+    def join(kv, first):
         for src in range(ny - 1):
             @pl.when(src < y)
             def _():
                 arrived(orecv.at[kv, src], o0 + kv * ny + src)
 
-    expand = jnp.where(
-        lax.rem(iota((tokens, 2 * rows), 1), rows) == lax.div(iota((tokens, 2 * rows), 0), POOL), 1.0, 0.0).astype(BF)
-    squares = jnp.zeros((tokens, HEAD), F32)
-    for w in range(2):
-        for kind in range(2):
-            kv = 2 * w + kind
-            for g in range(4):
-                part = slice(g * rows, (g + 1) * rows)
-                state = (mst[kv, 0, part], acc[kv, 0, part, :HEAD], acc[kv, 0, part, HEAD:])
-
-                def join(src, state):
-                    top, number, total = state
-                    stats = orecv[kv, src, :, 4 * HEAD:].astype(F32)
-                    other = stats[:, g:g + 1] + stats[:, 4 + g:5 + g] + stats[:, 8 + g:9 + g]
-                    other = jnp.broadcast_to(other, (rows, HEAD))
-                    newest = jnp.maximum(top, other)
-                    mine, theirs = jnp.exp2(top - newest), jnp.exp2(other - newest)
-                    blended = orecv[kv, src, :, g * HEAD:(g + 1) * HEAD].astype(F32)
-                    return newest, number * mine + blended * theirs, total * mine + theirs
-
-                top, number, total = lax.fori_loop(0, y, join, state)
-                coarse_out = jnp.where(total > 0.0, number / jnp.where(total > 0.0, total, 1.0), 0.0)
-                high, low = split_pair(coarse_out)
-                spread = dot(expand, jnp.concatenate([high, low], axis=0))
-                columns = slice((kv * 4 + g) * HEAD, (kv * 4 + g + 1) * HEAD)
-                lifted = (spread.reshape(tokens // 8, 8, HEAD) * both(up_ref[:, columns])[None]).reshape(tokens, HEAD)
-                combined = fine[:, columns] + lifted
-                fine[:, columns] = combined
-                squares = squares + combined * combined
-    ssq[...] = squares
+        squares = jnp.zeros((tokens, HEAD), F32) if first else ssq[...]
+        for g in range(4):
+            part = slice(g * rows, (g + 1) * rows)
+            state = (mst[kv, 0, part], acc[kv, 0, part, :HEAD], acc[kv, 0, part, HEAD:])
+
+            def add(src, state):
+                top, number, total = state
+                stats = orecv[kv, src, :, 4 * HEAD:].astype(F32)
+                other = stats[:, g:g + 1] + stats[:, 4 + g:5 + g] + stats[:, 8 + g:9 + g]
+                other = jnp.broadcast_to(other, (rows, HEAD))
+                newest = jnp.maximum(top, other)
+                mine, theirs = jnp.exp2(top - newest), jnp.exp2(other - newest)
+                blended = orecv[kv, src, :, g * HEAD:(g + 1) * HEAD].astype(F32)
+                return newest, number * mine + blended * theirs, total * mine + theirs
+
+            top, number, total = lax.fori_loop(0, y, add, state)
+            coarse_out = jnp.where(total > 0.0, number / jnp.where(total > 0.0, total, 1.0), 0.0)
+            high, low = split_pair(coarse_out)
+            spread = dot(expand, jnp.concatenate([high, low], axis=0))
+            columns = slice((kv * 4 + g) * HEAD, (kv * 4 + g + 1) * HEAD)
+            lifted = (spread.reshape(tokens // 8, 8, HEAD) * both(up_ref[:, columns])[None]).reshape(tokens, HEAD)
+            combined = fine[:, columns] + lifted
+            fine[:, columns] = combined
+            squares = squares + combined * combined
+        ssq[...] = squares
+
+    begun = set()
+
+    def is_first(name):
+        fresh = name not in begun
+        begun.add(name)
+        return fresh
+
+    near, far = (0, -1, 1, 2), (-2, 3, 4, 5)
+    plain = {
+        "hq": halo_queries, "BI": window_masks, "PQ": pool_queries,
+        "qs": query_start, "qr": query_relay, "qw": query_rest, "PR": prepare_rest,
+    }
+    for item in order.split():
+        number = [int(c) for c in item if c.isdigit()]
+        if item in plain:
+            plain[item]()
+        elif item[:2] in ("hs", "hr", "hw"):
+            {"hs": halo_start, "hr": halo_relay, "hw": halo_rest}[item[:2]]("kv".index(item[2]))
+        elif item[:2] == "as":
+            ax_start(*number)
+        elif item[:2] == "ar":
+            ax_rest(*number)
+        elif item[0] == "a":
+            az(*number)
+        elif item[0] == "B":
+            bz(*number)
+        elif item[0] == "b":
+            {"bs": bx_start, "br": bx_relay, "bw": bx_rest}[item[:2]](*number)
+        elif item[:2] == "UA":
+            coarse_a(number[0], far if number[1] else near, is_first(2 * number[0]))
+        elif item[:2] == "UB":
+            coarse_b(*number, is_first(2 * number[0] + 1))
+        elif item[0] == "F":
+            finish(*number)
+            send_partials(*number)
+        elif item[0] == "W":
+            window(*number)
+        else:
+            join(*number, is_first("join"))
+
     send(ssq, norm0, partner, ssq_in)
     arrived(ssq_in, norm0)
-    mean = jnp.sum(squares + ssq_in[...], axis=1, keepdims=True) / (2.0 * q_ref.shape[1])
+    mean = jnp.sum(ssq[...] + ssq_in[...], axis=1, keepdims=True) / (2.0 * q_ref.shape[1])
     factor = jnp.broadcast_to(lax.rsqrt(mean + 1e-05), (tokens, HEAD))
     for n in range(heads):
         columns = slice(n * HEAD, (n + 1) * HEAD)
@@ -492,10 +501,10 @@
     kv_width = keys.shape[1]
     rows = tokens // POOL
     kv_heads = kv_width // HEAD
-    sems = 2 * (3 + 2 * (nz - 1) + 6) + 5 + ny + 4 * ny + 1
+    sems = 2 * 3 + 5 * (nz - 1) + 4 * 3 + 5 + ny + 4 * ny + 1
     vmem = pl.BlockSpec(memory_space=pltpu.VMEM)
     return pl.pallas_call(
-        functools.partial(kernel, ny, nz),
+        functools.partial(kernel, ny, nz, " ".join(ORDER)),
         out_shape=jax.ShapeDtypeStruct((tokens, width), BF),
         in_specs=[vmem] * 8,
         out_specs=vmem,
@@ -524,7 +533,7 @@
             pltpu.SemaphoreType.DMA((sems,)),
             pltpu.SemaphoreType.DMA((sems,)),
         ],
-        compiler_params=pltpu.CompilerParams(collective_id=0, has_side_effects=True),
+        compiler_params=pltpu.CompilerParams(collective_id=0, has_side_effects=True, vmem_limit_bytes=36000000),
     )(queries, keys, values, qw, kw, vw, up, gain[None])
 
 

time: 88.7 us -> 88.3 us (level)
  the two profiles are of different devices: /device:TPU:31 before, /device:TPU:9 now
where the time goes in v3:
time: 88.3 us; the launch traced here: 87.9 us
  Pallas kernels  80.2 us (91%)
  local copies, waits for them, and re-layouts  7.7 us (9%)
    pallas_call x1, Pallas kernels, per_device(): pl.pallas_call(functools.partial(kernel, ny, nz, ' '.join(ORDER)), out_sh...  80.2 us
    unnamed x17, local copies, waits for them, and re-layouts  7.7 us

profile of v3, /device:TPU:9, one launch (start us, length us, event | category | flops | bytes accessed | tf_op | source)
XLA Modules:
  0.0 87.9 jit_solution(7023376421475711488)
XLA Ops:
  0.0 0.0 copy-start
  0.0 1.2 %copy-done = bf16[256,2048]{1,0:T(8,128)(2,1)S(1)} copy-done((bf16[256,2048]{1,0:T(8,128)(2,1)S(1)}, bf16[256,2048]{1,0:T(8,128)(2,1)}, u32[]{:S(2)}) %copy-start) | copy-done | bytes 1048600
  1.2 0.0 copy-start.1
  1.2 0.9 %copy-done.1 = bf16[256,512]{1,0:T(8,128)(2,1)S(1)} copy-done((bf16[256,512]{1,0:T(8,128)(2,1)S(1)}, bf16[256,512]{1,0:T(8,128)(2,1)}, u32[]{:S(2)}) %copy-start.1) | copy-done | bytes 262168
  2.2 0.0 copy-start.2
  2.2 0.9 %copy-done.2 = bf16[256,512]{1,0:T(8,128)(2,1)S(1)} copy-done((bf16[256,512]{1,0:T(8,128)(2,1)S(1)}, bf16[256,512]{1,0:T(8,128)(2,1)}, u32[]{:S(2)}) %copy-start.2) | copy-done | bytes 262168
  3.1 0.0 copy-start.3
  3.1 0.8 copy-done.3
  3.9 0.0 copy-start.4
  3.9 0.8 copy-done.4
  4.6 0.0 copy-start.5
  4.6 0.7 copy-done.5
  5.3 0.0 copy-start.6
  5.3 0.7 copy-done.6
  6.0 0.0 copy-start.7
  6.0 0.7 copy-done.7
  6.7 80.2 %shard_map.82 = bf16[256,2048]{1,0:T(8,128)(2,1)S(1)} custom-call(bf16[256,2048]{1,0:T(8,128)(2,1)S(1)} %copy-done, bf16[256,512]{1,0:T(8,128)(2,1)S(1)} %copy-done.1, bf16[256,512]{1,0:T(8,128)(2,1)S(1)} %copy-done.2, f32[4,2048]{1,0:T(4,128)S(1)} %copy-done.3, f32[4,512]{1,0:T(4,128)S(1)} %copy-done.5, f32[4,512]{1,0:T(4,128)S(1)} %copy-done.6, ...), custom_call_target="tpu_custom_call" | custom-call | tf_op jit(solution)/shard_map/pallas_call | solution.py:506
  86.9 1.0 %copy.10 = bf16[256,2048]{1,0:T(8,128)(2,1)} copy(bf16[256,2048]{1,0:T(8,128)(2,1)S(1)} %shard_map.82) | data formatting | bytes 2097152
Async XLA Ops:
  0.0 1.2 %copy-start = (bf16[256,2048]{1,0:T(8,128)(2,1)S(1)}, bf16[256,2048]{1,0:T(8,128)(2,1)}, u32[]{:S(2)}) copy-start(bf16[256,2048]{1,0:T(8,128)(2,1)} %q_ref.1) | copy-start | bytes 3145732
  1.2 0.9 %copy-start.1 = (bf16[256,512]{1,0:T(8,128)(2,1)S(1)}, bf16[256,512]{1,0:T(8,128)(2,1)}, u32[]{:S(2)}) copy-start(bf16[256,512]{1,0:T(8,128)(2,1)} %k_ref.1) | copy-start | bytes 786436
  2.2 0.9 %copy-start.2 = (bf16[256,512]{1,0:T(8,128)(2,1)S(1)}, bf16[256,512]{1,0:T(8,128)(2,1)}, u32[]{:S(2)}) copy-start(bf16[256,512]{1,0:T(8,128)(2,1)} %v_ref.1) | copy-start | bytes 786436
  3.1 0.8 copy-start.3
  3.9 0.8 copy-start.4
  4.6 0.7 copy-start.5
  5.3 0.7 copy-start.6
  6.0 0.7 copy-start.7

commit v4 on v3

--- a/solution.py
+++ b/solution.py
@@ -24,22 +24,23 @@
     "PQ B3 a010 hsv",
     "qs ar1 B4 a000",
     "a110 BI B5 a011",
-    "bs00 bs01 bs11 qr",
-    "a100 a001 br00 bs10",
-    "a111 a012 a101 a002",
-    "a013 a003 br01 hrv",
-    "qw PR hrk bw00",
-    "a102 a112 a014 UA00",
-    "br11 UB00 a004 a103",
-    "UA10 a113 bw01 br10",
-    "UB01 bw11 F1 a005",
-    "a015 UA01 hwv a114",
-    "a104 F0 bw10 UB10",
-    "UB11 hwk a115 a105",
-    "F3 UA11 F2 W2",
-    "W1 W0 W3 J1",
-    "J0 J2 J3",
+    "bs00 bs01 bs11 a100",
+    "a001 br00 bs10 a111",
+    "a012 a101 a002 a013",
+    "a003 br01 hrv qw",
+    "PR hrk bw00 a102",
+    "a112 a014 UA00 br11",
+    "UB00 a004 a103 UA10",
+    "a113 bw01 br10 UB01",
+    "bw11 F1 a005 a015",
+    "UA01 hwv a114 a104",
+    "F0 bw10 UB10 UB11",
+    "hwk a115 a105 F3",
+    "UA11 F2 W2 W1",
+    "W0 W3 J1 J0",
+    "J2 J3",
 )
+PIECES = 2
 
 
 def split_pair(value):
@@ -98,14 +99,14 @@
         return (lax.div(pp, ns), lax.rem(pp, ns), h)
 
     x_next, x_prev, x_far = wrap(x + 1, NX), wrap(x - 1, NX), wrap(x + 2, NX)
-    right, left = at(z, x_next), at(z, x_prev)
+    right, left, across = at(z, x_next), at(z, x_prev), at(z, x_far)
     above, below = at(wrap(z + 1, nz), x), at(wrap(z - 1, nz), x)
     following = at_position(lax.rem(position + 1, ny * ns))
     preceding = at_position(lax.rem(position + ny * ns - 1, ny * ns))
     partner = (y, s, 1 - h)
 
     barrier = pltpu.get_barrier_semaphore()
-    peers = [right, left, above, below, following, preceding, partner]
+    peers = [right, left, across, above, below, following, preceding, partner]
     peers += [(lax.rem(y + step, ny), s, h) for step in range(1, ny)]
     both = lambda w: jnp.concatenate([w, w], axis=0)
     for peer in peers:
@@ -152,11 +153,11 @@
         base = ax0 + 3 * w
         send(ga.at[w, z, x], base + 1, left)
         send(ga.at[w, z, x], base + 0, right)
+        send(ga.at[w, z, x], base + 2, across)
 
     def ax_rest(w):
         base = ax0 + 3 * w
         arrived(ga.at[w, z, x_next], base + 1)
-        send(ga.at[w, z, x_next], base + 2, left)
         arrived(ga.at[w, z, x_prev], base + 0)
         arrived(ga.at[w, z, x_far], base + 2)
 
@@ -174,7 +175,7 @@
                 send(ref_at(wrap(z - d, nz)), base + d, above)
 
     def az(w, part, d):
-        along_z(lambda zz: ga.at[w, zz, pl.ds(part * (NX // 2), NX // 2)], az0 + (2 * w + part) * (nz - 1), d)
+        along_z(lambda zz: ga.at[w, zz, pl.ds(part * (NX // PIECES), NX // PIECES)], az0 + (2 * w + part) * (nz - 1), d)
 
     def bz(d):
         along_z(lambda zz: gb.at[:, x, zz], bz0, d)
@@ -252,38 +253,20 @@
 
         lax.fori_loop(0, heads // 2, two_heads, 0)
 
-    def query_copy(t, target, index):
-        return remote(qall.at[t], qall.at[t], q0 + index, q0 + t, (target, s, h))
+    def query_copy(step):
+        return remote(qall.at[y], qall.at[y], q0 + step, q0 + y, (y - step, s, h))
 
     def query_start():
-        @pl.when(y > 0)
-        def _():
-            query_copy(y, y - 1, 0).start()
-
-        @pl.when(y == ny - 1)
-        def _():
-            query_copy(y, 0, 1).start()
-
-    def query_relay():
-        @pl.when(y == 1)
-        def _():
-            arrived(qall.at[2], q0 + 2)
-            query_copy(2, 0, 2).start()
-
-        @pl.when(y == 0)
-        def _():
-            arrived(qall.at[ny - 1], q0 + ny - 1)
-            query_copy(ny - 1, 1, 2).start()
+        for step in (1, ny - 1) + tuple(range(2, ny - 1)):
+            @pl.when(y >= step)
+            def _():
+                query_copy(step).start()
 
     def query_rest():
-        @pl.when(y == 0)
-        def _():
-            arrived(qall.at[1], q0 + 1)
-            arrived(qall.at[2], q0 + 2)
-
-        @pl.when((y == 1) | (y == 2))
-        def _():
-            arrived(qall.at[ny - 1], q0 + ny - 1)
+        for t in range(1, ny):
+            @pl.when(t > y)
+            def _():
+                arrived(qall.at[t], q0 + t)
 
     def prepare_rest():
         for j in range(1, ny):
@@ -432,7 +415,7 @@
     near, far = (0, -1, 1, 2), (-2, 3, 4, 5)
     plain = {
         "hq": halo_queries, "BI": window_masks, "PQ": pool_queries,
-        "qs": query_start, "qr": query_relay, "qw": query_rest, "PR": prepare_rest,
+        "qs": query_start, "qw": query_rest, "PR": prepare_rest,
     }
     for item in order.split():
         number = [int(c) for c in item if c.isdigit()]
@@ -472,21 +455,10 @@
 
     for copy in unconditional:
         copy.wait_send()
-    @pl.when(y > 0)
-    def _():
-        query_copy(y, y - 1, 0).wait_send()
-
-    @pl.when(y == ny - 1)
-    def _():
-        query_copy(y, 0, 1).wait_send()
-
-    @pl.when(y == 1)
-    def _():
-        query_copy(2, 0, 2).wait_send()
-
-    @pl.when(y == 0)
-    def _():
-        query_copy(ny - 1, 1, 2).wait_send()
+    for step in range(1, ny):
+        @pl.when(y >= step)
+        def _():
+            query_copy(step).wait_send()
 
     for kv in range(4):
         for j in range(1, ny):
@@ -533,7 +505,7 @@
             pltpu.SemaphoreType.DMA((sems,)),
             pltpu.SemaphoreType.DMA((sems,)),
         ],
-        compiler_params=pltpu.CompilerParams(collective_id=0, has_side_effects=True, vmem_limit_bytes=36000000),
+        compiler_params=pltpu.CompilerParams(collective_id=0, has_side_effects=True),
     )(queries, keys, values, qw, kw, vw, up, gain[None])
 
 

time: 88.3 us -> 78.9 us (0.89)
  the two profiles are of different devices: /device:TPU:9 before, /device:TPU:31 now
where the time goes in v4:
time: 78.9 us; the launch traced here: 78.7 us
  Pallas kernels  76.4 us (97%)
  local copies, waits for them, and re-layouts  2.3 us (3%)
    pallas_call x1, Pallas kernels, per_device(): pl.pallas_call(functools.partial(kernel, ny, nz, ' '.join(ORDER)), out_sh...  76.4 us
    unnamed x1, local copies, waits for them, and re-layouts  2.3 us

profile of v4, /device:TPU:31, one launch (start us, length us, event | category | flops | bytes accessed | tf_op | source)
XLA Modules:
  0.0 78.7 jit_solution(7805919243059667683)
XLA Ops:
  0.0 76.4 %shard_map.82 = bf16[256,2048]{1,0:T(8,128)(2,1)} custom-call(bf16[256,2048]{1,0:T(8,128)(2,1)} %q_ref.1, bf16[256,512]{1,0:T(8,128)(2,1)} %k_ref.1, bf16[256,512]{1,0:T(8,128)(2,1)} %v_ref.1, f32[4,2048]{1,0:T(4,128)} %qw_ref.1, f32[4,512]{1,0:T(4,128)} %kw_ref.1, f32[4,512]{1,0:T(4,128)} %vw_ref.1, f32[4,2048]{1,0:T(4,128)} %up_ref.1, f32[1,2048]{1,0:T(1,128)} %bitcast.1), custom_call_target="tpu_custom_call" | custom-call | tf_op jit(solution)/shard_map/pallas_call | solution.py:478
  76.4 2.3 %copy.10 = bf16[256,2048]{1,0:T(8,128)(2,1)} copy(bf16[256,2048]{1,0:T(8,128)(2,1)} %shard_map.82) | data formatting | bytes 2097152

commit v5 on v4

--- a/solution.py
+++ b/solution.py
@@ -27,16 +27,16 @@
     "bs00 bs01 bs11 a100",
     "a001 br00 bs10 a111",
     "a012 a101 a002 a013",
-    "a003 br01 hrv qw",
-    "PR hrk bw00 a102",
-    "a112 a014 UA00 br11",
-    "UB00 a004 a103 UA10",
+    "a003 br01 qw PR",
+    "bw00 a102 a112 hrk",
+    "a014 UA00 br11 UB00",
+    "a004 a103 hrv UA10",
     "a113 bw01 br10 UB01",
     "bw11 F1 a005 a015",
-    "UA01 hwv a114 a104",
-    "F0 bw10 UB10 UB11",
-    "hwk a115 a105 F3",
-    "UA11 F2 W2 W1",
+    "UA01 a114 a104 F0",
+    "bw10 UB10 UB11 F3",
+    "a115 a105 UA11 F2",
+    "hwk hwv W2 W1",
     "W0 W3 J1 J0",
     "J2 J3",
 )
@@ -380,29 +380,36 @@
                 arrived(orecv.at[kv, src], o0 + kv * ny + src)
 
         squares = jnp.zeros((tokens, HEAD), F32) if first else ssq[...]
-        for g in range(4):
-            part = slice(g * rows, (g + 1) * rows)
-            state = (mst[kv, 0, part], acc[kv, 0, part, :HEAD], acc[kv, 0, part, HEAD:])
+        for pair in (0, 2):
+            def part_of(g):
+                return slice(g * rows, (g + 1) * rows)
+
+            state = tuple(
+                (mst[kv, 0, part_of(g)], acc[kv, 0, part_of(g), :HEAD], acc[kv, 0, part_of(g), HEAD:])
+                for g in (pair, pair + 1))
 
             def add(src, state):
-                top, number, total = state
                 stats = orecv[kv, src, :, 4 * HEAD:].astype(F32)
-                other = stats[:, g:g + 1] + stats[:, 4 + g:5 + g] + stats[:, 8 + g:9 + g]
-                other = jnp.broadcast_to(other, (rows, HEAD))
-                newest = jnp.maximum(top, other)
-                mine, theirs = jnp.exp2(top - newest), jnp.exp2(other - newest)
-                blended = orecv[kv, src, :, g * HEAD:(g + 1) * HEAD].astype(F32)
-                return newest, number * mine + blended * theirs, total * mine + theirs
-
-            top, number, total = lax.fori_loop(0, y, add, state)
-            coarse_out = jnp.where(total > 0.0, number / jnp.where(total > 0.0, total, 1.0), 0.0)
-            high, low = split_pair(coarse_out)
-            spread = dot(expand, jnp.concatenate([high, low], axis=0))
-            columns = slice((kv * 4 + g) * HEAD, (kv * 4 + g + 1) * HEAD)
-            lifted = (spread.reshape(tokens // 8, 8, HEAD) * both(up_ref[:, columns])[None]).reshape(tokens, HEAD)
-            combined = fine[:, columns] + lifted
-            fine[:, columns] = combined
-            squares = squares + combined * combined
+                joined = []
+                for g, (top, number, total) in zip((pair, pair + 1), state):
+                    other = stats[:, g:g + 1] + stats[:, 4 + g:5 + g] + stats[:, 8 + g:9 + g]
+                    other = jnp.broadcast_to(other, (rows, HEAD))
+                    newest = jnp.maximum(top, other)
+                    mine, theirs = jnp.exp2(top - newest), jnp.exp2(other - newest)
+                    blended = orecv[kv, src, :, g * HEAD:(g + 1) * HEAD].astype(F32)
+                    joined.append((newest, number * mine + blended * theirs, total * mine + theirs))
+                return tuple(joined)
+
+            done = lax.fori_loop(0, y, add, state)
+            for g, (top, number, total) in zip((pair, pair + 1), done):
+                coarse_out = jnp.where(total > 0.0, number / jnp.where(total > 0.0, total, 1.0), 0.0)
+                high, low = split_pair(coarse_out)
+                spread = dot(expand, jnp.concatenate([high, low], axis=0))
+                columns = slice((kv * 4 + g) * HEAD, (kv * 4 + g + 1) * HEAD)
+                lifted = (spread.reshape(tokens // 8, 8, HEAD) * both(up_ref[:, columns])[None]).reshape(tokens, HEAD)
+                combined = fine[:, columns] + lifted
+                fine[:, columns] = combined
+                squares = squares + combined * combined
         ssq[...] = squares
 
     begun = set()

time: 78.9 us -> 77 us (0.976)
  the two profiles are of different devices: /device:TPU:31 before, /device:TPU:17 now
where the time goes in v5:
time: 77 us; the launch traced here: 76.9 us
  Pallas kernels  74.6 us (97%)
  local copies, waits for them, and re-layouts  2.3 us (3%)
    pallas_call x1, Pallas kernels, per_device(): pl.pallas_call(functools.partial(kernel, ny, nz, ' '.join(ORDER)), out_sh...  74.6 us
    unnamed x1, local copies, waits for them, and re-layouts  2.3 us

profile of v5, /device:TPU:17, one launch (start us, length us, event | category | flops | bytes accessed | tf_op | source)
XLA Modules:
  0.0 76.9 jit_solution(14758848490194654856)
XLA Ops:
  0.0 74.6 %shard_map.82 = bf16[256,2048]{1,0:T(8,128)(2,1)} custom-call(bf16[256,2048]{1,0:T(8,128)(2,1)} %q_ref.1, bf16[256,512]{1,0:T(8,128)(2,1)} %k_ref.1, bf16[256,512]{1,0:T(8,128)(2,1)} %v_ref.1, f32[4,2048]{1,0:T(4,128)} %qw_ref.1, f32[4,512]{1,0:T(4,128)} %kw_ref.1, f32[4,512]{1,0:T(4,128)} %vw_ref.1, f32[4,2048]{1,0:T(4,128)} %up_ref.1, f32[1,2048]{1,0:T(1,128)} %bitcast.1), custom_call_target="tpu_custom_call" | custom-call | tf_op jit(solution)/shard_map/pallas_call | solution.py:485
  74.6 2.3 %copy.10 = bf16[256,2048]{1,0:T(8,128)(2,1)} copy(bf16[256,2048]{1,0:T(8,128)(2,1)} %shard_map.82) | data formatting | bytes 2097152
